TPU v7x, 128 devices: a whole 4x4x4 slice. The times are simulated.
128 devices in a mesh: dom: 4 (over x), tile: 32 (over y, z, core).
Axes of the slice: x: 4, y: 4, z: 4, core: 2. Of those that a mesh axis runs over, the one named last changes fastest.
Arguments:
- atm_anom: bfloat16 [512, 80, 127, 128], P(('dom', 'tile')), may hold values from -0.25 to 0.25
- ocn_anom: bfloat16 [512, 80, 75, 128], P(('dom', 'tile')), may hold values from -0.25 to 0.25
- atm_vec: bfloat16 [512, 127, 128], P(('dom', 'tile')), may hold values from -6 to 6
- ocn_vec: bfloat16 [512, 75, 128], P(('dom', 'tile')), may hold values from -6 to 6
- atm_to_ocean: int32 [512, 128], P(('dom', 'tile')), may hold values from 0 to 65535, as said below
- sea_tiles: int32 [512], P(('dom', 'tile')), may hold values 0 or 1
- atm_class: int32 [512, 5], P(('dom', 'tile')), may hold values from 0 to 4
- ocn_class: int32 [512, 5], P(('dom', 'tile')), may hold values from 0 to 4
Outputs:
- atm_out: float32 [512, 127, 128], P(('dom', 'tile'))
- ocn_out: float32 [512, 75, 128], P(('dom', 'tile'))
Inputs may be any that keep to these rules, and one draw needn't show every extreme that they name: atm_to_ocean is one to one onto all 65536 ocean columns; the atmosphere columns held by the r-th device along dom+tile (tiles r * 4 to r * 4 + 3) are paired exactly with the ocean columns whose column index c satisfies c // (128 / number of devices) = r.
All inputs are finite; a program needn't handle non-finite values. No bound on the sum of `sea_tiles` on one device may be relied on, other than what follows from the above.
Results may differ from a plain program's by a relative error of at most 0.0029.
Values may be sent and summed in bfloat16 or wider, within the bound.
A program may use at most 64 MiB of HBM per device.

v0:
```python
import jax
import jax.numpy as jnp
from jax import lax
from jax.sharding import PartitionSpec as P

KA = 16
KO = 16
HALO = 2


COUPLING = 8.0
ATM_SPREAD = 12.0
OCN_SPREAD = 8.0
CLASS_TABLE = (1.0, 0.7, 0.45, 0.25, 0.0)


def padded_2(block, sides, width):
    for axis, dim in sides:
        count = lax.axis_size(axis)
        forward = [(i, i + 1) for i in range(count - 1)]
        forward.append((count - 1, 0))
        backward = [(target, source) for source, target in forward]
        low = lax.ppermute(
            lax.slice_in_dim(block, block.shape[dim] - width, None, axis=dim), axis, forward
        )
        high = lax.ppermute(lax.slice_in_dim(block, 0, width, axis=dim), axis, backward)
        block = jnp.concatenate([low, block, high], axis=dim)
    return block


def level_taper(level_count, spread):
    position = jnp.arange(level_count, dtype=jnp.float32)
    scaled = (position[:, None] - position[None, :]) / spread
    return jnp.exp(-0.5 * scaled * scaled)


def class_weights(classes):
    class_table = jnp.array(CLASS_TABLE, jnp.float32)
    matches = classes[..., None] == jnp.arange(len(CLASS_TABLE), dtype=jnp.int32)
    return jnp.sum(jnp.where(matches, class_table, 0.0), axis=-1)


def spread_tiles(padded, classes, tile_count):
    weights = class_weights(classes)
    summed = jnp.zeros((tile_count,) + padded.shape[1:], jnp.float32)
    for offset in range(2 * HALO + 1):
        summed = summed + weights[:, offset, None, None] * padded[offset : offset + tile_count]
    return summed


def vertical(spread, tapering):
    return jnp.einsum("tmk,lk->tml", spread, tapering, precision=lax.Precision.HIGHEST).astype(
        jnp.bfloat16
    )


def local(atm_anom, ocn_anom, atm_vec, ocn_vec, atm_to_ocean, sea_tiles, atm_class, ocn_class):
    tile_count, members, atm_levels, columns = atm_anom.shape
    ocn_levels = ocn_anom.shape[2]
    device_count = lax.axis_size("dom") * lax.axis_size("tile")
    per_peer = columns // device_count
    flat_width = tile_count * columns
    surface_start = atm_levels - KA
    rise_position = jnp.arange(KA, dtype=jnp.float32)
    rise_weights = jnp.exp(-2.0 * (KA - 1 - rise_position) / KA)
    fall_position = jnp.arange(KO, dtype=jnp.float32)
    fall_weights = jnp.exp(-2.0 * fall_position / KO)
    sea_flags = sea_tiles.astype(jnp.float32)
    target = atm_to_ocean.reshape(flat_width)
    ocean_tile = target // columns
    ocean_column = target % columns
    slot_index = (
        ocean_tile % tile_count * columns
        + ocean_tile // tile_count * per_peer
        + ocean_column % per_peer
    )
    slot_source = (
        jnp.zeros_like(slot_index).at[slot_index].set(jnp.arange(flat_width, dtype=jnp.int32))
    )
    atm_surface = atm_anom[:, :, surface_start:, :]
    ocn_top = ocn_anom[:, :, :KO, :]
    atm_coeff = jnp.einsum("tmlc,tlc->tml", atm_anom, atm_vec, preferred_element_type=jnp.float32)
    ocn_coeff = (
        jnp.einsum("tmlc,tlc->tml", ocn_anom, ocn_vec, preferred_element_type=jnp.float32)
        * sea_flags[:, None, None]
    )
    joined = jnp.concatenate([atm_coeff, ocn_coeff], axis=2)
    padded = padded_2(joined, (("tile", 0),), HALO)
    atm_weighted = atm_vec[:, surface_start:, :].astype(jnp.float32) * rise_weights[None, :, None]
    atm_proj = jnp.einsum("tmsc,tsc->mtc", atm_surface.astype(jnp.float32), atm_weighted).astype(
        jnp.bfloat16
    )
    outgoing = jnp.take(atm_proj.reshape(members, flat_width), slot_source, axis=1).reshape(
        members, tile_count, columns
    )
    ocean_proj = lax.all_to_all(outgoing, ("dom", "tile"), split_axis=2, concat_axis=2, tiled=True)
    ocn_weighted = (
        ocn_vec[:, :KO, :].astype(jnp.float32)
        * fall_weights[None, :, None]
        * sea_flags[:, None, None]
    )
    ocn_proj = jnp.einsum("tmoc,toc->mtc", ocn_top.astype(jnp.float32), ocn_weighted).astype(
        jnp.bfloat16
    )
    returned = lax.all_to_all(ocn_proj, ("dom", "tile"), split_axis=2, concat_axis=2, tiled=True)
    atm_pair = jnp.take(returned.reshape(members, flat_width), slot_index, axis=1).reshape(
        members, tile_count, columns
    )
    ocean_proj, atm_pair = (ocean_proj, atm_pair)
    atm_spread = spread_tiles(padded[:, :, :atm_levels], atm_class, tile_count)
    ocn_spread = spread_tiles(padded[:, :, atm_levels:], ocn_class, tile_count)
    atm_vertical = vertical(atm_spread, level_taper(atm_levels, ATM_SPREAD))
    ocn_vertical = vertical(ocn_spread, level_taper(ocn_levels, OCN_SPREAD))
    atm_out = jnp.einsum(
        "tmlc,tml->tlc", atm_anom, atm_vertical, preferred_element_type=jnp.float32
    )
    atm_cross = (
        jnp.einsum("tmsc,mtc->tsc", atm_surface, atm_pair, preferred_element_type=jnp.float32)
        * (COUPLING * rise_weights)[None, :, None]
    )
    atm_out = atm_out.at[:, surface_start:, :].add(atm_cross)
    ocean_paired = jnp.transpose(ocean_proj, (1, 0, 2))

    def second_pass(anomaly, vertical_coeff, paired):
        intra_part = jnp.einsum(
            "mlc,ml->lc", anomaly, vertical_coeff, preferred_element_type=jnp.float32
        )
        cross_part = (
            jnp.einsum("moc,mc->oc", anomaly[:, :KO], paired, preferred_element_type=jnp.float32)
            * (COUPLING * fall_weights)[:, None]
        )
        return intra_part.at[:KO].add(cross_part)

    ocn_out = jax.vmap(second_pass)(ocn_anom, ocn_vertical, ocean_paired) * sea_flags[:, None, None]
    return (atm_out, ocn_out)


def solution(mesh):
    in_specs = (
        P(("dom", "tile"), None, None, None),
        P(("dom", "tile"), None, None, None),
        P(("dom", "tile"), None, None),
        P(("dom", "tile"), None, None),
        P(("dom", "tile"), None),
        P(("dom", "tile")),
        P(("dom", "tile"), None),
        P(("dom", "tile"), None),
    )
    out_specs = (P(("dom", "tile"), None, None), P(("dom", "tile"), None, None))
    return jax.shard_map(local, mesh=mesh, in_specs=in_specs, out_specs=out_specs, check_vma=False)
```

profile of v0, /device:TPU:0, one launch (start us, length us, event | category | flops | bytes accessed | tf_op | source)
XLA Modules:
  0.0 73.2 jit_solution(6392722483695629167)
XLA Ops:
  0.6 6.1 %fusion.22 = f32[4,75,1,80]{3,2,1,0:T(1,128)S(1)} fusion(bf16[4,80,75,128]{3,1,2,0:T(8,128)(2,1)} %param.17, bf16[4,75,128,1]{2,0,1,3:T(4,128)(2,1)} %bitcast.119), kind=kOutput, calls=%fused_computation.41 | convolution fusion | flops 6144000 | bytes 6316800 | tf_op jit(solution)/shard_map/tmlc,tlc->tml/dot_general | solution.py:84
  6.7 0.1 copy.21
  6.9 0.0 copy-start.2
  6.9 0.0 copy-start.3
  6.9 0.0 copy-start.4
  6.9 0.0 copy-start.5
  7.0 8.0 %fusion.2 = f32[4,127,1,80]{3,2,1,0:T(1,128)S(1)} fusion(bf16[4,80,127,128]{3,1,2,0:T(8,128)(2,1)} %param.16, bf16[4,127,128,1]{2,0,1,3:T(4,128)(2,1)S(1)} %bitcast.116), kind=kOutput, calls=%fused_computation.16 | convolution fusion | flops 10403840 | bytes 10696448 | tf_op jit(solution)/shard_map/tmlc,tlc->tml/dot_general | solution.py:82
  15.0 0.2 copy.19
  15.2 0.1 fusion.19
  15.2 0.1 fusion.4
  15.4 0.1 collective-permute-start
  15.5 6.1 %collective-permute-start.1 = (f32[2,80,202]{2,1,0:T(8,128)S(1)}, f32[2,80,202]{2,1,0:T(8,128)S(1)}, u32[]{:S(2)}, u32[]{:S(2)}) collective-permute-start(f32[2,80,202]{2,1,0:T(8,128)S(1)} %get-tuple-element.34), channel_id=1, source_target_pairs={{1,0},{2,1},{3,2},{4,3},{5,4},{6,5},{7,6},{8,7},{9,8},{10,9},{11,1... | collective-permute-start | bytes 387848 | tf_op jit(solution)/shard_map/ppermute | solution.py:26
  21.6 0.8 %multiply_bitcast_fusion.1 = f32[4,128,16]{1,0,2:T(4,128)S(1)} fusion(f32[4]{0:T(128)S(1)} %convert_element_type.29, f32[16]{0:T(128)S(1)} %multiply_exponential_fusion.1, bf16[4,75,128]{2,0,1:T(4,128)(2,1)} %param.19), kind=kLoop, calls=%fused_computation.80 | loop fusion | flops 24576 | bytes 49232
  22.4 1.6 %multiply_reduce_fusion.3 = bf16[4,128,80]{1,2,0:T(8,128)(2,1)S(1)} fusion(f32[4,128,16]{1,2,0:T(8,128)S(1)} %copy.58, bf16[4,80,75,128]{3,1,2,0:T(8,128)(2,1)} %param.17), kind=kLoop, calls=%fused_computation.6 | loop fusion | flops 1925120 | bytes 1425408
  24.0 0.8 %copy.66 = bf16[4,128,80]{2,0,1:T(4,128)(2,1)} copy(bf16[4,128,80]{1,2,0:T(8,128)(2,1)S(1)} %multiply_reduce_fusion.3) | data formatting | bytes 163840
  24.8 6.8 %all-to-all-start = ((bf16[80,4,128]{0,1,2:T(4,128)(2,1)}), bf16[80,4,128]{0,1,2:T(4,128)(2,1)S(1)}, u32[]{:S(2)}, u32[]{:S(2)}) async-start(bf16[80,4,128]{0,1,2:T(4,128)(2,1)} %bitcast.24), calls=%async_computation | async-start | bytes 262144 | tf_op jit(solution)/shard_map/all_to_all | solution.py:105
  31.7 2.4 %scatter_custom_fusion = s32[512]{0:T(512)S(1)} fusion(s32[512]{0:T(512)S(1)} %bitcast.122, s32[512]{0:T(512)S(1)} %iota.42, s32[]{:T(128)} %constant.148.clone.1), kind=kCustom, calls=%fused_computation.126 | custom fusion | bytes 2052 | tf_op jit(solution)/shard_map/scatter | solution.py:78
  34.2 0.1 copy.16
  34.3 0.1 copy.14
  34.4 0.1 multiply_bitcast_fusion
  34.5 1.6 %multiply_reduce_fusion.1 = bf16[4,128,80]{1,2,0:T(8,128)(2,1)S(1)} fusion(f32[4,128,16]{1,2,0:T(8,128)S(1)} %copy.60, bf16[4,80,127,128]{3,1,2,0:T(8,128)(2,1)} %param.16), kind=kLoop, calls=%fused_computation.4 | loop fusion | flops 1925120 | bytes 1425408
  36.1 0.1 copy.49
  36.3 1.3 %gather_fusion.1 = bf16[512,80]{1,0:T(8,128)(2,1)S(1)} fusion(bf16[80,512]{0,1:T(8,128)(2,1)S(1)} %bitcast.112, s32[1024]{0:T(1024)S(1)} %pad_clamp_fusion), kind=kCustom, calls=%fused_computation.1.clone | custom fusion | bytes 165888 | tf_op jit(solution)/shard_map/jit(_take)/gather | solution.py:93
  37.6 0.1 broadcast_select_fusion
  37.8 0.8 %copy.17 = bf16[80,4,128]{0,1,2:T(4,128)(2,1)} copy(bf16[80,4,128]{0,2,1:T(8,128)(2,1)S(1)} %bitcast.117) | data formatting | bytes 163840 | tf_op jit(solution)/shard_map/reshape | solution.py:93
  38.5 0.2 select_reduce_fusion
  38.7 2.5 %all-to-all-done = bf16[80,4,128]{0,1,2:T(4,128)(2,1)S(1)} async-done(((bf16[80,4,128]{0,1,2:T(4,128)(2,1)}), bf16[80,4,128]{0,1,2:T(4,128)(2,1)S(1)}, u32[]{:S(2)}, u32[]{:S(2)}) %all-to-all-start) | async-done | bytes 81952 | tf_op jit(solution)/shard_map/all_to_all | solution.py:105
  41.2 7.4 %all-to-all-start.1 = ((bf16[80,4,128]{0,1,2:T(4,128)(2,1)}), bf16[80,4,128]{0,1,2:T(4,128)(2,1)S(1)}, u32[]{:S(2)}, u32[]{:S(2)}) async-start(bf16[80,4,128]{0,1,2:T(4,128)(2,1)} %copy.17), calls=%async_computation.1 | async-start | bytes 262144 | tf_op jit(solution)/shard_map/all_to_all | solution.py:96
  48.7 1.3 %gather_fusion = bf16[512,80]{1,0:T(8,128)(2,1)S(1)} fusion(bf16[80,512]{0,1:T(8,128)(2,1)S(1)} %bitcast.111, s32[1024]{0:T(1024)S(1)} %pad_clamp_fusion.1), kind=kCustom, calls=%fused_computation.clone | custom fusion | bytes 165888 | tf_op jit(solution)/shard_map/jit(_take)/gather | solution.py:106
  50.1 0.1 broadcast_select_fusion.1
  50.2 0.1 copy.59
  50.3 1.7 %multiply_reduce_fusion.2 = f32[4,128,16]{1,2,0:T(8,128)S(1)} fusion(f32[4,128,80]{1,2,0:T(8,128)S(1)} %copy.59, bf16[4,80,127,128]{3,1,2,0:T(8,128)(2,1)} %param.16), kind=kLoop, calls=%fused_computation.5 | loop fusion | flops 1957888 | bytes 1507328
  52.0 6.1 %all-to-all-done.1 = bf16[80,4,128]{0,1,2:T(4,128)(2,1)S(1)} async-done(((bf16[80,4,128]{0,1,2:T(4,128)(2,1)}), bf16[80,4,128]{0,1,2:T(4,128)(2,1)S(1)}, u32[]{:S(2)}, u32[]{:S(2)}) %all-to-all-start.1) | async-done | bytes 81952 | tf_op jit(solution)/shard_map/all_to_all | solution.py:96
  58.1 0.1 copy.61
  58.3 1.7 %multiply_reduce_fusion = f32[4,128,16]{1,2,0:T(8,128)S(1)} fusion(f32[4,128,80]{1,2,0:T(8,128)S(1)} %copy.61, bf16[4,80,75,128]{3,1,2,0:T(8,128)(2,1)} %param.17), kind=kLoop, calls=%fused_computation.3 | loop fusion | flops 1957888 | bytes 1507328
  60.0 0.2 maximum_maximum_fusion
  60.2 0.4 fusion
  60.6 0.2 copy.22
  60.8 5.5 %fusion.72 = f32[4,127,1,128]{3,2,1,0:T(1,128)S(1)} fusion(bf16[4,80,127,1]{1,3,2,0:T(2,128)(2,1)S(1)} %copy.22, bf16[4,80,127,128]{3,1,2,0:T(8,128)(2,1)} %param.16), kind=kOutput, calls=%fused_computation.147 | convolution fusion | flops 10403840 | bytes 10745216 | tf_op jit(solution)/shard_map/tmlc,tml->tlc/dot_general | solution.py:114
  66.3 0.1 copy.79
  66.4 0.5 fusion.1
  66.9 0.2 copy.40
  67.0 4.4 %fusion.73 = f32[4,75,1,128]{3,2,1,0:T(1,128)S(1)} fusion(bf16[4,80,75,1]{1,3,2,0:T(2,128)(2,1)S(1)} %copy.40, bf16[4,80,75,128]{3,1,2,0:T(8,128)(2,1)} %param.17), kind=kOutput, calls=%fused_computation.148 | convolution fusion | flops 6144000 | bytes 6345600 | tf_op jit(solution)/shard_map/vmap(mlc,ml->lc)/dot_general | solution.py:125
  71.5 0.1 copy.80
  71.5 0.1 fusion.50
  71.6 0.8 %broadcast_multiply_fusion = f32[4,75,128]{2,0,1:T(4,128)} fusion(f32[4,75,128]{2,0,1:T(4,128)S(1)} %fusion.50, f32[4]{0:T(128)S(1)} %convert_element_type.29), kind=kLoop, calls=%fused_computation.56 | loop fusion | flops 38400 | bytes 307216 | tf_op jit(solution)/shard_map/mul | solution.py:134
  72.4 0.1 fusion.51
  72.5 0.7 copy-done.1
  (28 shorter events, 0.2 us)
Async XLA Ops:
  0.6 6.2 %copy-start.6 = (s32[4]{0:T(128)S(1)}, s32[4]{0:T(128)}, u32[]{:S(2)}) copy-start(s32[4]{0:T(128)} %param.21) | copy-start | bytes 52
  0.6 6.3 %copy-start = (bf16[4,127,128]{2,0,1:T(4,128)(2,1)S(1)}, bf16[4,127,128]{2,0,1:T(4,128)(2,1)}, u32[]{:S(2)}) copy-start(bf16[4,127,128]{2,0,1:T(4,128)(2,1)} %param.18) | copy-start | bytes 390148
  6.9 24.7 %copy-start.2 = (s32[4,128]{1,0:T(4,128)S(1)}, s32[4,128]{1,0:T(4,128)}, u32[]{:S(2)}) copy-start(s32[4,128]{1,0:T(4,128)} %param.20) | copy-start | bytes 6148
  6.9 27.3 %copy-start.3 = (s32[4,5]{1,0:T(4,128)S(1)}, s32[4,5]{1,0:T(4,128)}, u32[]{:S(2)}) copy-start(s32[4,5]{1,0:T(4,128)} %param.23) | copy-start | bytes 244
  6.9 27.4 %copy-start.4 = (s32[4,5]{1,0:T(4,128)S(1)}, s32[4,5]{1,0:T(4,128)}, u32[]{:S(2)}) copy-start(s32[4,5]{1,0:T(4,128)} %param.22) | copy-start | bytes 244
  6.9 31.6 %copy-start.5 = (f32[5]{0:T(128)S(1)}, f32[5]{0:T(128)}, u32[]{:S(2)}) copy-start(f32[5]{0:T(128)} %constant.162.clone) | copy-start | bytes 64
  15.4 44.6 %collective-permute-start = (f32[2,80,202]{2,1,0:T(8,128)S(1)}, f32[2,80,202]{2,1,0:T(8,128)S(1)}, u32[]{:S(2)}, u32[]{:S(2)}) collective-permute-start(f32[2,80,202]{2,1,0:T(8,128)S(1)} %get-tuple-element.33), channel_id=1, source_target_pairs={{0,1},{1,2},{2,3},{3,4},{4,5},{5,6},{6,7},{7,8},{8,9},{9,10},{10,1... | collective-permute-start | bytes 387848 | tf_op jit(solution)/shard_map/ppermute | solution.py:23
  15.5 44.5 %collective-permute-start.1 = (f32[2,80,202]{2,1,0:T(8,128)S(1)}, f32[2,80,202]{2,1,0:T(8,128)S(1)}, u32[]{:S(2)}, u32[]{:S(2)}) collective-permute-start(f32[2,80,202]{2,1,0:T(8,128)S(1)} %get-tuple-element.34), channel_id=1, source_target_pairs={{1,0},{2,1},{3,2},{4,3},{5,4},{6,5},{7,6},{8,7},{9,8},{10,9},{11,1... | collective-permute-start | bytes 387848 | tf_op jit(solution)/shard_map/ppermute | solution.py:26
  24.8 16.4 %all-to-all-start = ((bf16[80,4,128]{0,1,2:T(4,128)(2,1)}), bf16[80,4,128]{0,1,2:T(4,128)(2,1)S(1)}, u32[]{:S(2)}, u32[]{:S(2)}) async-start(bf16[80,4,128]{0,1,2:T(4,128)(2,1)} %bitcast.24), calls=%async_computation | async-start | bytes 262144 | tf_op jit(solution)/shard_map/all_to_all | solution.py:105
  41.2 16.9 %all-to-all-start.1 = ((bf16[80,4,128]{0,1,2:T(4,128)(2,1)}), bf16[80,4,128]{0,1,2:T(4,128)(2,1)S(1)}, u32[]{:S(2)}, u32[]{:S(2)}) async-start(bf16[80,4,128]{0,1,2:T(4,128)(2,1)} %copy.17), calls=%async_computation.1 | async-start | bytes 262144 | tf_op jit(solution)/shard_map/all_to_all | solution.py:96
  72.5 0.7 copy-start.1
where the time goes:
time: 74 us; the launch traced here: 73.2 us
  matrix products  24.9 us (34%)
  starting transfers between devices  20.4 us (28%)
  other arithmetic  9.51 us (13%)
  local copies, waits for them, and re-layouts  8.77 us (12%)
  waiting for transfers between devices  8.62 us (12%)
  between operations  0.99 us (1%)
    dot_general x1, matrix products, local(): jnp.einsum('tmlc,tlc->tml', atm_anom, atm_vec, preferred_element_type=jnp...  8.04 us
    unnamed x7, other arithmetic  7.51 us
    all_to_all x1, starting transfers between devices, local(): lax.all_to_all(outgoing, ('dom', 'tile'), split_axis=2, concat_axis=2, ti...  7.45 us
    all_to_all x1, starting transfers between devices, local(): lax.all_to_all(ocn_proj, ('dom', 'tile'), split_axis=2, concat_axis=2, ti...  6.8 us
    ppermute x1, starting transfers between devices, padded_2(): lax.ppermute(lax.slice_in_dim(block, 0, width, axis=dim), axis, backward)  6.11 us
    all_to_all x1, waiting for transfers between devices, local(): lax.all_to_all(outgoing, ('dom', 'tile'), split_axis=2, concat_axis=2, ti...  6.1 us
    dot_general x1, matrix products, local(): jnp.einsum('tmlc,tlc->tml', ocn_anom, ocn_vec, preferred_element_type=jnp...  6.07 us
    dot_general x1, matrix products, local(): jnp.einsum('tmlc,tml->tlc', atm_anom, atm_vertical, preferred_element_typ...  5.49 us
  transfers between devices with their start and end apart: 4, of which 2 were waited for; matrix products, arithmetic and copies ran while one was open for 21% of the time, Pallas kernels for 0%

commit v1 on v0

v1 whole, which is shorter than its diff:
```python
import functools

import jax
import jax.numpy as jnp
import numpy as np
from jax import lax
from jax.experimental import pallas as pl
from jax.experimental.pallas import tpu as pltpu
from jax.sharding import PartitionSpec as P

M = 80
LA = 127
LO = 75
C = 128
KA = 16
KO = 16
TD = 4
BLOCK = 16
SURF = LA - KA
ROWS_A = 128
ROWS_O = 80
HALO_ROWS = ROWS_A + ROWS_O
PEERS = 128
PER_PEER = 8
ROUTE = PEERS * PER_PEER

COUPLING = 8.0
CLASS_TABLE = (1.0, 0.7, 0.45, 0.25, 0.0)
RISE = [float(np.exp(np.float32(-2.0 * (KA - 1 - s) / KA))) for s in range(KA)]
FALL = [float(np.exp(np.float32(-2.0 * o / KO))) for o in range(KO)]

F32 = jnp.float32
BF16 = jnp.bfloat16
MESH = pl.DeviceIdType.MESH


def class_weight(code):
    weight = jnp.float32(CLASS_TABLE[-1])
    for index in range(len(CLASS_TABLE) - 1):
        weight = jnp.where(code == index, jnp.float32(CLASS_TABLE[index]), weight)
    return weight


def taper_split(rows, levels, spread):
    row = lax.broadcasted_iota(jnp.int32, (rows, rows), 0)
    col = lax.broadcasted_iota(jnp.int32, (rows, rows), 1)
    scaled = (row - col).astype(F32) / spread
    full = jnp.exp(-0.5 * scaled * scaled)
    full = jnp.where((row < levels) & (col < levels), full, 0.0)
    high = full.astype(BF16)
    low = (full - high.astype(F32)).astype(BF16)
    return high, low


def dot(a, b):
    return lax.dot_general(a, b, (((1,), (0,)), ((), ())), preferred_element_type=F32)


def dot_nt(a, b):
    return lax.dot_general(a, b, (((1,), (1,)), ((), ())), preferred_element_type=F32)


def dot_tn(a, b):
    return lax.dot_general(a, b, (((0,), (0,)), ((), ())), preferred_element_type=F32)


def peer_of(step, me_dom, me_tile):
    def reach(k):
        return jnp.where(k < 2, k + 2, 3 - k)

    y, z, core = me_tile // 8, (me_tile // 2) % 4, me_tile % 2
    dom = (me_dom + reach(step // 32)) % 4
    y = (y + reach((step // 8) % 4)) % 4
    z = (z + reach((step // 2) % 4)) % 4
    core = (core + 1 - step % 2) % 2
    return dom, (y * 4 + z) * 2 + core


def kernel(
    atm_hbm, ocn_hbm, avec_hbm, ovec_hbm, pair_hbm, sea, acls, ocls, aout, oout,
    atm, ocn, avec, ovec, pairing, avf, ovf, send_map, recv_map, proj, outgoing, incoming,
    coeff_a, coeff_o, vert_a, vert_o, halo_out, halo_in, paired,
    load_sems, small_sems, send_sem, recv_sem, own_sem, halo_send, halo_recv,
):
    me_dom, me_tile = lax.axis_index("dom"), lax.axis_index("tile")
    me = me_dom * 32 + me_tile

    def small_loads():
        return [
            pltpu.make_async_copy(avec_hbm, avec, small_sems.at[0]),
            pltpu.make_async_copy(ovec_hbm, ovec, small_sems.at[1]),
            pltpu.make_async_copy(pair_hbm, pairing, small_sems.at[2]),
        ]

    def surface_loads():
        return [
            pltpu.make_async_copy(
                ocn_hbm.at[:, pl.ds(0, KO)], ocn.at[:, pl.ds(0, KO)], load_sems.at[0]
            ),
            pltpu.make_async_copy(
                atm_hbm.at[:, pl.ds(SURF, KA)], atm.at[:, pl.ds(SURF, KA)], load_sems.at[1]
            ),
        ]

    def tile_loads(t):
        return [
            pltpu.make_async_copy(
                atm_hbm.at[t, pl.ds(0, SURF)], atm.at[t, pl.ds(0, SURF)], load_sems.at[2 + 2 * t]
            ),
            pltpu.make_async_copy(
                ocn_hbm.at[t, pl.ds(KO, LO - KO)],
                ocn.at[t, pl.ds(KO, LO - KO)],
                load_sems.at[3 + 2 * t],
            ),
        ]

    for copy in small_loads() + surface_loads():
        copy.start()
    for t in range(TD):
        for copy in tile_loads(t):
            copy.start()

    barrier = pltpu.get_barrier_semaphore()

    def greet(step, carry):
        dom, tile = peer_of(step, me_dom, me_tile)
        pl.semaphore_signal(barrier, inc=1, device_id=(dom, tile), device_id_type=MESH)
        return carry

    lax.fori_loop(0, PEERS - 1, greet, 0)

    coeff_a[...] = jnp.zeros_like(coeff_a)
    coeff_o[...] = jnp.zeros_like(coeff_o)
    proj[pl.ds(M, C - M), :] = jnp.zeros((C - M, 2 * TD * C), BF16)

    for copy in small_loads():
        copy.wait()
    avf[...] = avec[...].astype(F32)
    ovf[...] = ovec[...].astype(F32)

    lane = lax.broadcasted_iota(jnp.int32, (1, C), 1)

    def build_maps(b, carry):
        start = pl.multiple_of(b * C, C)
        row = lax.broadcasted_iota(jnp.int32, (C, C), 0) + start
        for t in range(TD):
            slot = lax.shift_right_logical(pairing[pl.ds(t, 1), :], 7)
            spot = lax.shift_right_logical(slot, 2) * PER_PEER + (slot & 3)
            cols = pl.ds(t * C, C)
            send_map[pl.ds(start, C), cols] = jnp.where(row == spot, 1.0, 0.0).astype(BF16)
            recv_map[pl.ds(start, C), cols] = jnp.where(row == spot + 4, 1.0, 0.0).astype(BF16)
            cols = pl.ds((TD + t) * C, C)
            spot = lane * PER_PEER + t
            send_map[pl.ds(start, C), cols] = jnp.where(row == spot + 4, 1.0, 0.0).astype(BF16)
            recv_map[pl.ds(start, C), cols] = jnp.where(row == spot, 1.0, 0.0).astype(BF16)
        return carry

    lax.fori_loop(0, ROUTE // C, build_maps, 0)

    for copy in surface_loads():
        copy.wait()
    for t in range(TD):
        total = jnp.zeros((M, C), F32)
        for o in range(KO):
            row = ovf[o, pl.ds(t, 1), :] * FALL[o]
            total = total + ocn[t, o].astype(F32) * row
        wet = sea[t].astype(F32)
        proj[pl.ds(0, M), pl.ds((TD + t) * C, C)] = (total * wet).astype(BF16)
        total = jnp.zeros((M, C), F32)
        for s in range(KA):
            row = avf[SURF + s, pl.ds(t, 1), :] * RISE[s]
            total = total + atm[t, SURF + s].astype(F32) * row
        proj[pl.ds(0, M), pl.ds(t * C, C)] = total.astype(BF16)

    def fill_outgoing(b, carry):
        rows = dot_nt(send_map[pl.ds(pl.multiple_of(b * C, C), C), :], proj[...])
        outgoing[pl.ds(b * (C // PER_PEER), C // PER_PEER)] = rows.astype(BF16).reshape(
            C // PER_PEER, PER_PEER, C
        )
        return carry

    lax.fori_loop(0, ROUTE // C, fill_outgoing, 0)

    pl.semaphore_wait(barrier, PEERS - 1)

    own = pltpu.make_async_copy(outgoing.at[me], incoming.at[me], own_sem)
    own.start()

    def push(step, carry):
        dom, tile = peer_of(step, me_dom, me_tile)
        pltpu.make_async_remote_copy(
            src_ref=outgoing.at[dom * 32 + tile],
            dst_ref=incoming.at[me],
            send_sem=send_sem,
            recv_sem=recv_sem,
            device_id=(dom, tile),
            device_id_type=MESH,
        ).start()
        return carry

    lax.fori_loop(0, PEERS - 1, push, 0)

    ahigh, alow = taper_split(ROWS_A, LA, 12.0)
    ohigh, olow = taper_split(ROWS_O, LO, 8.0)
    sub = lax.broadcasted_iota(jnp.int32, (8, M), 0)

    def coeff_block(anom, vec, coeff, t, first):
        rows = vec[pl.ds(first, BLOCK), t, :].astype(BF16)
        halves = [jnp.zeros((8, M), F32)] * 2
        for j in range(BLOCK):
            out = dot_nt(rows, anom[t, first + j])
            half = j // 8
            halves[half] = jnp.where(sub == j % 8, out[half * 8 : half * 8 + 8], halves[half])
        coeff[pl.ds(first, 8), pl.ds(0, M)] = halves[0]
        coeff[pl.ds(first + 8, 8), pl.ds(0, M)] = halves[1]

    def tapered(high, low, coeff):
        value = coeff[...]
        top = value.astype(BF16)
        rest = (value - top.astype(F32)).astype(BF16)
        return dot(high, top) + dot(high, rest) + dot(low, top)

    def halo_copy(side):
        step = 31 if side == 0 else 1
        return pltpu.make_async_remote_copy(
            src_ref=halo_out.at[side],
            dst_ref=halo_in.at[side],
            send_sem=halo_send.at[side],
            recv_sem=halo_recv.at[side],
            device_id=(me_dom, (me_tile + step) % 32),
            device_id_type=MESH,
        )

    for t in range(TD):
        for copy in tile_loads(t):
            copy.wait()

        def atm_block(b, carry, t=t):
            coeff_block(atm, avf, coeff_a, t, b * BLOCK)
            return carry

        def ocn_block(b, carry, t=t):
            coeff_block(ocn, ovf, coeff_o, t, b * BLOCK)
            return carry

        lax.fori_loop(0, LA // BLOCK, atm_block, 0)
        coeff_block(atm, avf, coeff_a, t, LA - BLOCK)
        lax.fori_loop(0, LO // BLOCK, ocn_block, 0)
        coeff_block(ocn, ovf, coeff_o, t, LO - BLOCK)
        wet = sea[t].astype(F32)
        tap_a = tapered(ahigh, alow, coeff_a)
        tap_o = tapered(ohigh, olow, coeff_o) * wet
        vert_a[t] = tap_a
        vert_o[t] = tap_o
        halo_out[t // 2, t % 2, pl.ds(0, ROWS_A), :] = tap_a.astype(BF16)
        halo_out[t // 2, t % 2, pl.ds(ROWS_A, ROWS_O), :] = tap_o.astype(BF16)
        if t % 2 == 1:
            halo_copy(t // 2).start()

    for side in range(2):
        halo_copy(side).wait_recv()

    def neighbour(own, first, rows, index):
        if index < 0:
            return halo_in[1, index + 2, pl.ds(first, rows), :].astype(F32)
        if index >= TD:
            return halo_in[0, index - TD, pl.ds(first, rows), :].astype(F32)
        return own[index]

    def spread(own, codes, first, rows):
        results = []
        for t in range(TD):
            total = jnp.zeros((rows, C), F32)
            for d in range(5):
                total = total + class_weight(codes[t, d]) * neighbour(own, first, rows, t + d - 2)
            results.append(total)
        for t in range(TD):
            own[t] = results[t]

    spread(vert_a, acls, 0, ROWS_A)
    spread(vert_o, ocls, ROWS_A, ROWS_O)

    sub_c = lax.broadcasted_iota(jnp.int32, (8, C), 0)

    def out_block(anom, vert, out, t, first, scale):
        rows = vert[t, pl.ds(first, BLOCK), pl.ds(0, M)].astype(BF16)
        halves = [jnp.zeros((8, C), F32)] * 2
        for j in range(BLOCK):
            value = dot(rows, anom[t, first + j])
            half = j // 8
            halves[half] = jnp.where(sub_c == j % 8, value[half * 8 : half * 8 + 8], halves[half])
        for half in range(2):
            out[pl.ds(first + half * 8, 8), t, :] = halves[half] * scale

    for t in range(TD):
        wet = sea[t].astype(F32)

        def atm_second(b, carry, t=t):
            out_block(atm, vert_a, aout, t, b * BLOCK, 1.0)
            return carry

        def ocn_second(b, carry, t=t, wet=wet):
            out_block(ocn, vert_o, oout, t, b * BLOCK, wet)
            return carry

        lax.fori_loop(0, LA // BLOCK, atm_second, 0)
        out_block(atm, vert_a, aout, t, LA - BLOCK, 1.0)
        lax.fori_loop(0, LO // BLOCK, ocn_second, 0)
        out_block(ocn, vert_o, oout, t, LO - BLOCK, wet)

    own.wait()
    everyone = pltpu.make_async_remote_copy(
        src_ref=outgoing.at[pl.ds(0, PEERS - 1)],
        dst_ref=incoming.at[pl.ds(0, PEERS - 1)],
        send_sem=send_sem,
        recv_sem=recv_sem,
        device_id=(me_dom, (me_tile + 1) % 32),
        device_id_type=MESH,
    )
    everyone.wait_recv()
    arrived = incoming[...].reshape(ROUTE, C)
    for half in range(2):
        cols = pl.ds(half * TD * C, TD * C)
        paired[:, cols] = dot_tn(arrived, recv_map[:, cols])[:M]

    for t in range(TD):
        wet = sea[t].astype(F32)
        own_pair = paired[:, pl.ds(t * C, C)]
        for s in range(KA):
            cross = jnp.sum(atm[t, SURF + s].astype(F32) * own_pair, axis=0, keepdims=True)
            aout[SURF + s, pl.ds(t, 1), :] += cross * (COUPLING * RISE[s])
        own_pair = paired[:, pl.ds((TD + t) * C, C)]
        for o in range(KO):
            cross = jnp.sum(ocn[t, o].astype(F32) * own_pair, axis=0, keepdims=True)
            oout[o, pl.ds(t, 1), :] += cross * (COUPLING * FALL[o]) * wet

    everyone.wait_send()
    for side in range(2):
        halo_copy(side).wait_send()


def local(atm_anom, ocn_anom, atm_vec, ocn_vec, atm_to_ocean, sea_tiles, atm_class, ocn_class):
    hbm = pl.BlockSpec(memory_space=pl.ANY)
    smem = pl.BlockSpec(memory_space=pltpu.SMEM)
    vmem = pl.BlockSpec(memory_space=pltpu.VMEM)
    dma = pltpu.SemaphoreType.DMA
    atm_out, ocn_out = pl.pallas_call(
        kernel,
        out_shape=(
            jax.ShapeDtypeStruct((LA, TD, C), F32),
            jax.ShapeDtypeStruct((LO, TD, C), F32),
        ),
        in_specs=[hbm] * 5 + [smem] * 3,
        out_specs=(vmem, vmem),
        scratch_shapes=[
            pltpu.VMEM((TD, LA, M, C), BF16),
            pltpu.VMEM((TD, LO, M, C), BF16),
            pltpu.VMEM((LA, TD, C), BF16),
            pltpu.VMEM((LO, TD, C), BF16),
            pltpu.VMEM((TD, C), jnp.int32),
            pltpu.VMEM((LA, TD, C), F32),
            pltpu.VMEM((LO, TD, C), F32),
            pltpu.VMEM((ROUTE, 2 * TD * C), BF16),
            pltpu.VMEM((ROUTE, 2 * TD * C), BF16),
            pltpu.VMEM((C, 2 * TD * C), BF16),
            pltpu.VMEM((PEERS, PER_PEER, C), BF16),
            pltpu.VMEM((PEERS, PER_PEER, C), BF16),
            pltpu.VMEM((ROWS_A, C), F32),
            pltpu.VMEM((ROWS_O, C), F32),
            pltpu.VMEM((TD, ROWS_A, C), F32),
            pltpu.VMEM((TD, ROWS_O, C), F32),
            pltpu.VMEM((2, 2, HALO_ROWS, C), BF16),
            pltpu.VMEM((2, 2, HALO_ROWS, C), BF16),
            pltpu.VMEM((M, 2 * TD * C), F32),
            dma((2 + 2 * TD,)),
            dma((3,)),
            dma,
            dma,
            dma,
            dma((2,)),
            dma((2,)),
        ],
        compiler_params=pltpu.CompilerParams(
            collective_id=0, has_side_effects=True, vmem_limit_bytes=40 * 1024 * 1024
        ),
    )(
        jnp.transpose(atm_anom, (0, 2, 1, 3)),
        jnp.transpose(ocn_anom, (0, 2, 1, 3)),
        jnp.transpose(atm_vec, (1, 0, 2)),
        jnp.transpose(ocn_vec, (1, 0, 2)),
        atm_to_ocean,
        sea_tiles,
        atm_class,
        ocn_class,
    )
    return jnp.transpose(atm_out, (1, 0, 2)), jnp.transpose(ocn_out, (1, 0, 2))


def solution(mesh):
    both = ("dom", "tile")
    in_specs = (
        P(both, None, None, None),
        P(both, None, None, None),
        P(both, None, None),
        P(both, None, None),
        P(both, None),
        P(both),
        P(both, None),
        P(both, None),
    )
    out_specs = (P(both, None, None), P(both, None, None))
    return jax.shard_map(local, mesh=mesh, in_specs=in_specs, out_specs=out_specs, check_vma=False)
```

time: 74 us -> 63.3 us (0.86)
  Pallas kernels: 0 us -> 53.8 us
  matrix products: 24.9 us -> 0 us
  starting transfers between devices: 20.4 us -> 0 us
  other arithmetic: 9.51 us -> 0 us
  waiting for transfers between devices: 8.62 us -> 0 us
    pallas_call x0 -> x1, Pallas kernels: none -> 53.8 us  [local(): pl.pallas_call(kernel, out_shape=(jax.ShapeDtypeStruct((LA, TD, C), F32),...]
    dot_general x6 -> x0, matrix products: 24.9 us -> none  [the longest x1 8.04 us: local(): jnp.einsum('tmlc,tlc->tml', atm_anom, atm_vec, preferred_element_type=jnp...]
    all_to_all x2 -> x0, starting transfers between devices: 14.2 us -> none  [the longest x1 7.45 us: local(): lax.all_to_all(outgoing, ('dom', 'tile'), split_axis=2, concat_axis=2, ti...]
    all_to_all x2 -> x0, waiting for transfers between devices: 8.61 us -> none  [the longest x1 6.1 us: local(): lax.all_to_all(outgoing, ('dom', 'tile'), split_axis=2, concat_axis=2, ti...]
    unnamed x7 -> x0, other arithmetic: 7.51 us -> none
    unnamed x21 -> x16, local copies, waits for them, and re-layouts: 1.93 us -> 8.58 us
    ppermute x2 -> x0, starting transfers between devices: 6.18 us -> none  [the longest x1 6.11 us: padded_2(): lax.ppermute(lax.slice_in_dim(block, 0, width, axis=dim), axis, backward)]
    gather x2 -> x0, local copies, waits for them, and re-layouts: 2.68 us -> none  [the longest x1 1.34 us: local(): jnp.take(returned.reshape(members, flat_width), slot_index, axis=1)]
  transfers between devices with their start and end apart: 4 -> 0, of which waited for: 2 -> 0; matrix products, arithmetic and copies ran while one was open for 21% -> 0% of each run, Pallas kernels for 0% -> 0%
where the time goes in v1:
time: 63.3 us; the launch traced here: 63 us
  Pallas kernels  53.8 us (85%)
  local copies, waits for them, and re-layouts  8.58 us (14%)
  between operations  0.66 us (1%)
    pallas_call x1, Pallas kernels, local(): pl.pallas_call(kernel, out_shape=(jax.ShapeDtypeStruct((LA, TD, C), F32),...  53.8 us
    unnamed x16, local copies, waits for them, and re-layouts  8.58 us

profile of v1, /device:TPU:0, one launch (start us, length us, event | category | flops | bytes accessed | tf_op | source)
XLA Modules:
  0.0 63.0 jit_solution(32046853175019481)
XLA Ops:
  0.6 0.0 copy-start
  0.6 2.7 %copy-done = bf16[4,80,75,128]{3,1,2,0:T(8,128)(2,1)S(1)} copy-done((bf16[4,80,75,128]{3,1,2,0:T(8,128)(2,1)S(1)}, bf16[4,80,75,128]{3,1,2,0:T(8,128)(2,1)}, u32[]{:S(2)}) %copy-start) | copy-done | bytes 6144024
  3.4 0.0 copy-start.1
  3.4 0.9 %copy-done.1 = bf16[4,127,128]{2,0,1:T(4,128)(2,1)S(1)} copy-done((bf16[4,127,128]{2,0,1:T(4,128)(2,1)S(1)}, bf16[4,127,128]{2,0,1:T(4,128)(2,1)}, u32[]{:S(2)}) %copy-start.1) | copy-done | bytes 130072
  4.3 0.0 copy-start.2
  4.3 0.9 %copy-done.2 = bf16[4,75,128]{2,0,1:T(4,128)(2,1)S(1)} copy-done((bf16[4,75,128]{2,0,1:T(4,128)(2,1)S(1)}, bf16[4,75,128]{2,0,1:T(4,128)(2,1)}, u32[]{:S(2)}) %copy-start.2) | copy-done | bytes 76824
  5.2 0.0 copy-start.3
  5.2 0.7 %copy-done.3 = s32[4,128]{1,0:T(4,128)S(1)} copy-done((s32[4,128]{1,0:T(4,128)S(1)}, s32[4,128]{1,0:T(4,128)}, u32[]{:S(2)}) %copy-start.3) | copy-done | bytes 2072
  5.8 0.0 copy-start.4
  5.9 0.7 %copy-done.4 = s32[4,5]{1,0:T(4,128)S(1)} copy-done((s32[4,5]{1,0:T(4,128)S(1)}, s32[4,5]{1,0:T(4,128)}, u32[]{:S(2)}) %copy-start.4) | copy-done | bytes 104
  6.5 0.0 copy-start.5
  6.5 0.7 %copy-done.5 = s32[4,5]{1,0:T(4,128)S(1)} copy-done((s32[4,5]{1,0:T(4,128)S(1)}, s32[4,5]{1,0:T(4,128)}, u32[]{:S(2)}) %copy-start.5) | copy-done | bytes 104
  7.2 0.0 copy-start.6
  7.2 0.7 %copy-done.6 = s32[4]{0:T(128)S(1)} copy-done((s32[4]{0:T(128)S(1)}, s32[4]{0:T(128)}, u32[]{:S(2)}) %copy-start.6) | copy-done | bytes 40
  7.9 53.8 %shard_map.95 = (f32[127,4,128]{2,1,0:T(4,128)S(1)}, f32[75,4,128]{2,1,0:T(4,128)S(1)}) custom-call(bf16[4,127,80,128]{3,2,1,0:T(8,128)(2,1)} %bitcast.11, bf16[4,75,80,128]{3,2,1,0:T(8,128)(2,1)S(1)} %bitcast.6, bf16[127,4,128]{2,1,0:T(4,128)(2,1)S(1)} %bitcast.9, bf16[75,4,128]{2,1,0:T(4,128)(2,1)S(1)} %bitcast.10, s32[4,128]{1,0:T(4,128)S(1)} %copy-done.3, ...), custom_call_target="tpu_custom_call" | custom-call | tf_op jit(solution)/shard_map/pallas_call | solution.py:347
  61.6 0.7 %copy.12 = f32[4,127,128]{2,0,1:T(4,128)} copy(f32[4,127,128]{2,0,1:T(4,128)S(1)} %bitcast.7) | data formatting | bytes 520192
  62.3 0.7 %copy.13 = f32[4,75,128]{2,0,1:T(4,128)} copy(f32[4,75,128]{2,0,1:T(4,128)S(1)} %bitcast.8) | data formatting | bytes 307200
Async XLA Ops:
  0.6 2.7 %copy-start = (bf16[4,80,75,128]{3,1,2,0:T(8,128)(2,1)S(1)}, bf16[4,80,75,128]{3,1,2,0:T(8,128)(2,1)}, u32[]{:S(2)}) copy-start(bf16[4,80,75,128]{3,1,2,0:T(8,128)(2,1)} %param.9) | copy-start | bytes 18432004
  3.4 0.9 %copy-start.1 = (bf16[4,127,128]{2,0,1:T(4,128)(2,1)S(1)}, bf16[4,127,128]{2,0,1:T(4,128)(2,1)}, u32[]{:S(2)}) copy-start(bf16[4,127,128]{2,0,1:T(4,128)(2,1)} %param.10) | copy-start | bytes 390148
  4.3 0.9 %copy-start.2 = (bf16[4,75,128]{2,0,1:T(4,128)(2,1)S(1)}, bf16[4,75,128]{2,0,1:T(4,128)(2,1)}, u32[]{:S(2)}) copy-start(bf16[4,75,128]{2,0,1:T(4,128)(2,1)} %param.11) | copy-start | bytes 230404
  5.2 0.7 %copy-start.3 = (s32[4,128]{1,0:T(4,128)S(1)}, s32[4,128]{1,0:T(4,128)}, u32[]{:S(2)}) copy-start(s32[4,128]{1,0:T(4,128)} %pair_hbm.1) | copy-start | bytes 6148
  5.8 0.7 %copy-start.4 = (s32[4,5]{1,0:T(4,128)S(1)}, s32[4,5]{1,0:T(4,128)}, u32[]{:S(2)}) copy-start(s32[4,5]{1,0:T(4,128)} %acls.1) | copy-start | bytes 244
  6.5 0.7 %copy-start.5 = (s32[4,5]{1,0:T(4,128)S(1)}, s32[4,5]{1,0:T(4,128)}, u32[]{:S(2)}) copy-start(s32[4,5]{1,0:T(4,128)} %ocls.1) | copy-start | bytes 244
  7.2 0.7 %copy-start.6 = (s32[4]{0:T(128)S(1)}, s32[4]{0:T(128)}, u32[]{:S(2)}) copy-start(s32[4]{0:T(128)} %sea.1) | copy-start | bytes 52

commit v2 on v1

v2 whole, which is shorter than its diff:
```python
import functools

import jax
import jax.numpy as jnp
import numpy as np
from jax import lax
from jax.experimental import pallas as pl
from jax.experimental.pallas import tpu as pltpu
from jax.sharding import PartitionSpec as P

M = 80
LA = 127
LO = 75
C = 128
KA = 16
KO = 16
TD = 4
BLOCK = 16
SURF = LA - KA
ROWS_A = 128
ROWS_O = 80
HALO_ROWS = ROWS_A + ROWS_O
PEERS = 128
PER_PEER = 8
ROUTE = PEERS * PER_PEER
SLOTS = TD * C
GROUP = 4
UNROLL = 9

COUPLING = 8.0
CLASS_TABLE = (1.0, 0.7, 0.45, 0.25, 0.0)
RISE = [float(np.exp(np.float32(-2.0 * (KA - 1 - s) / KA))) for s in range(KA)]
FALL = [float(np.exp(np.float32(-2.0 * o / KO))) for o in range(KO)]

F32 = jnp.float32
BF16 = jnp.bfloat16
LOGICAL = pl.DeviceIdType.LOGICAL


def class_weight(code):
    weight = jnp.float32(CLASS_TABLE[-1])
    for index in range(len(CLASS_TABLE) - 1):
        weight = jnp.where(code == index, jnp.float32(CLASS_TABLE[index]), weight)
    return weight


def taper_split(rows, levels, spread):
    row = lax.broadcasted_iota(jnp.int32, (rows, rows), 0)
    col = lax.broadcasted_iota(jnp.int32, (rows, rows), 1)
    scaled = (row - col).astype(F32) / spread
    full = jnp.exp(-0.5 * scaled * scaled)
    full = jnp.where((row < levels) & (col < levels), full, 0.0)
    high = full.astype(BF16)
    low = (full - high.astype(F32)).astype(BF16)
    return high, low


def dot(a, b):
    return lax.dot_general(a, b, (((1,), (0,)), ((), ())), preferred_element_type=F32)


def dot_nt(a, b):
    return lax.dot_general(a, b, (((1,), (1,)), ((), ())), preferred_element_type=F32)


def dot_tn(a, b):
    return lax.dot_general(a, b, (((0,), (0,)), ((), ())), preferred_element_type=F32)


def wrap(index, size):
    return jnp.where(index >= size, index - size, index)


def for_peers(me, action):
    def several(step, carry):
        for k in range(UNROLL):
            action(wrap(me + 1 + step * UNROLL + k, PEERS))
        return carry

    lax.fori_loop(0, (PEERS - 1) // UNROLL, several, 0)
    action(wrap(me + PEERS - 1, PEERS))


def lanes_sum(x):
    return jnp.sum(x, axis=1, keepdims=True)


def kernel(
    atm_hbm, ocn_hbm, avec_hbm, ovec_hbm, pair_hbm, sea, acls, ocls, aout, oout,
    atm, ocn, avec, ovec, pairing, avf, ovf, slot_map, proj_a, routed, outgoing, incoming,
    coeff_a, coeff_o, vert_a, vert_o, halo_out, halo_in, paired,
    load_sems, small_sems, send_sem, recv_sem, own_sem, halo_send, halo_recv,
):
    me_dom, me_tile = lax.axis_index("dom"), lax.axis_index("tile")
    me = me_dom * 32 + me_tile

    def small_loads():
        return [
            pltpu.make_async_copy(pair_hbm, pairing, small_sems.at[2]),
            pltpu.make_async_copy(ovec_hbm, ovec, small_sems.at[1]),
            pltpu.make_async_copy(avec_hbm, avec, small_sems.at[0]),
        ]

    def surface_loads():
        return [
            pltpu.make_async_copy(
                ocn_hbm.at[:, pl.ds(0, KO)], ocn.at[:, pl.ds(0, KO)], load_sems.at[0]
            ),
            pltpu.make_async_copy(
                atm_hbm.at[:, pl.ds(SURF, KA)], atm.at[:, pl.ds(SURF, KA)], load_sems.at[1]
            ),
        ]

    def tile_loads(t):
        return [
            pltpu.make_async_copy(
                atm_hbm.at[t, pl.ds(0, SURF)], atm.at[t, pl.ds(0, SURF)], load_sems.at[2 + 2 * t]
            ),
            pltpu.make_async_copy(
                ocn_hbm.at[t, pl.ds(KO, LO - KO)],
                ocn.at[t, pl.ds(KO, LO - KO)],
                load_sems.at[3 + 2 * t],
            ),
        ]

    for copy in small_loads() + surface_loads():
        copy.start()
    for t in range(TD):
        for copy in tile_loads(t):
            copy.start()

    barrier = pltpu.get_barrier_semaphore()

    def greet(peer):
        pl.semaphore_signal(barrier, inc=1, device_id=peer, device_id_type=LOGICAL)

    for_peers(me, greet)

    proj_a[pl.ds(M, C - M), :] = jnp.zeros((C - M, SLOTS), BF16)
    lane = lax.broadcasted_iota(jnp.int32, (1, C), 1)
    lanes = lax.broadcasted_iota(jnp.int32, (M, C), 1)
    sub = lax.broadcasted_iota(jnp.int32, (8, C), 0)

    for copy in small_loads():
        copy.wait()
    avf[...] = avec[...].astype(F32).reshape(LA * TD, C)
    ovf[...] = ovec[...].astype(F32).reshape(LO * TD, C)

    def vector_rows(vec, t, first, count):
        return vec[pl.ds(first * TD + t, count, stride=TD), :]

    for t in range(TD):
        slot = lax.shift_right_logical(pairing[pl.ds(t, 1), :], 7)

        def one_hot(b, carry, t=t, slot=slot):
            start = pl.multiple_of(b * C, C)
            row = lax.broadcasted_iota(jnp.int32, (C, C), 0) + start
            slot_map[pl.ds(start, C), pl.ds(t * C, C)] = jnp.where(row == slot, 1.0, 0.0).astype(
                BF16
            )
            return carry

        lax.fori_loop(0, SLOTS // C, one_hot, 0)

    for copy in surface_loads():
        copy.wait()

    def surface(anom, vec, t, first, scale):
        rows = vector_rows(vec, t, first, KA)
        total = jnp.zeros((M, C), F32)
        found = jnp.zeros((M, C), F32)
        for s in range(KA):
            product = anom[t, first + s].astype(F32) * (rows[s : s + 1] * scale[s])
            total = total + product
            found = jnp.where(lanes == s, lanes_sum(product), found)
        undo = jnp.zeros((1, C), F32)
        for s in range(KA):
            undo = jnp.where(lane == s, 1.0 / scale[s], undo)
        return total, found * undo

    def surface_tile(t, carry):
        wet = sea[t].astype(F32)
        total, found = surface(ocn, ovf, t, 0, FALL)
        coeff_o[t] = found
        turned = jnp.transpose(total * wet)
        routed[pl.ds(TD + t, C, stride=PER_PEER), pl.ds(0, M)] = turned
        total, found = surface(atm, avf, t, SURF, RISE)
        coeff_a[t] = pltpu.roll(found, SURF, 1)
        proj_a[pl.ds(0, M), pl.ds(pl.multiple_of(t * C, C), C)] = total.astype(BF16)
        return carry

    lax.fori_loop(0, TD, surface_tile, 0)

    for b in range(SLOTS // C):
        rows = dot_nt(slot_map[pl.ds(b * C, C), :], proj_a[...])
        for q in range(C // TD):
            routed[pl.ds((b * (C // TD) + q) * PER_PEER, TD), :] = rows[q * TD : q * TD + TD]
    outgoing[...] = routed[...].astype(BF16).reshape(PEERS, PER_PEER, C)

    pl.semaphore_wait(barrier, PEERS - 1)

    own = pltpu.make_async_copy(outgoing.at[me], incoming.at[me], own_sem)
    own.start()

    def push(peer):
        pltpu.make_async_remote_copy(
            src_ref=outgoing.at[peer],
            dst_ref=incoming.at[me],
            send_sem=send_sem,
            recv_sem=recv_sem,
            device_id=peer,
            device_id_type=LOGICAL,
        ).start()

    for_peers(me, push)

    def coeff_block(anom, vec, coeff, t, first):
        rows = vector_rows(vec, t, first, BLOCK)
        spot = lax.broadcasted_iota(jnp.int32, (BLOCK, C), 0)
        left = jnp.where(spot < GROUP, rows, 0.0).astype(BF16)
        right = jnp.where((spot >= GROUP) & (spot < 2 * GROUP), rows, 0.0).astype(BF16)
        stack = jnp.concatenate(
            [
                anom[t, pl.ds(first, GROUP)].reshape(GROUP * M, C),
                anom[t, pl.ds(first + GROUP, GROUP)].reshape(GROUP * M, C),
            ],
            axis=1,
        )
        out = dot_nt(stack, jnp.concatenate([left, right], axis=1))
        out = jnp.concatenate([out, jnp.zeros((GROUP * M, C - BLOCK), F32)], axis=1)
        found = jnp.zeros((M, C), F32)
        for g in range(GROUP):
            found = jnp.where(
                (lanes == g) | (lanes == g + GROUP), out[g * M : (g + 1) * M], found
            )
        for j in range(2 * GROUP, BLOCK):
            product = anom[t, first + j].astype(F32) * rows[j : j + 1]
            found = jnp.where(lanes == j, lanes_sum(product), found)
        moved = pltpu.roll(found, first, 1)
        here = (lanes >= first) & (lanes < first + BLOCK)
        coeff[t] = jnp.where(here, moved, coeff[t])

    ahigh, alow = taper_split(ROWS_A, LA, 12.0)
    ohigh, olow = taper_split(C, LO, 8.0)

    def tapered(high, low, value):
        top = value.astype(BF16)
        rest = (value - top.astype(F32)).astype(BF16)
        return dot_nt(high, top) + dot_nt(high, rest) + dot_nt(low, top)

    def halo_copy(side):
        step = 31 if side == 0 else 1
        return pltpu.make_async_remote_copy(
            src_ref=halo_out.at[side],
            dst_ref=halo_in.at[side],
            send_sem=halo_send.at[side],
            recv_sem=halo_recv.at[side],
            device_id=me_dom * 32 + wrap(me_tile + step, 32),
            device_id_type=LOGICAL,
        )

    def first_pass(t, carry):
        def atm_block(b, inner):
            coeff_block(atm, avf, coeff_a, t, jnp.minimum(b * BLOCK, SURF - BLOCK))
            return inner

        def ocn_block(b, inner):
            coeff_block(ocn, ovf, coeff_o, t, KO + jnp.minimum(b * BLOCK, LO - KO - BLOCK))
            return inner

        lax.fori_loop(0, pl.cdiv(SURF, BLOCK), atm_block, 0)
        lax.fori_loop(0, pl.cdiv(LO - KO, BLOCK), ocn_block, 0)
        wet = sea[t].astype(F32)
        tap_a = tapered(ahigh, alow, coeff_a[t])
        tap_o = tapered(ohigh[:ROWS_O], olow[:ROWS_O], coeff_o[t]) * wet
        vert_a[t] = tap_a
        vert_o[t] = tap_o
        side, place = t // 2, t % 2
        halo_out[side, place, pl.ds(0, ROWS_A), :] = tap_a.astype(BF16)
        halo_out[side, place, pl.ds(ROWS_A, ROWS_O), :] = tap_o.astype(BF16)
        return carry

    for side in range(2):
        for t in (2 * side, 2 * side + 1):
            for copy in tile_loads(t):
                copy.wait()
        lax.fori_loop(2 * side, 2 * side + 2, first_pass, 0)
        halo_copy(side).start()

    own.wait()
    everyone = pltpu.make_async_remote_copy(
        src_ref=outgoing.at[pl.ds(0, PEERS - 1)],
        dst_ref=incoming.at[pl.ds(0, PEERS - 1)],
        send_sem=send_sem,
        recv_sem=recv_sem,
        device_id=me_dom * 32 + wrap(me_tile + 1, 32),
        device_id_type=LOGICAL,
    )
    everyone.wait_recv()
    everyone.wait_send()
    routed[...] = incoming[...].astype(F32).reshape(ROUTE, C)
    for t in range(TD):
        turned = jnp.transpose(routed[pl.ds(t, C, stride=PER_PEER), :])
        paired[:, pl.ds((TD + t) * C, C)] = turned[:M]
    for_atm = jnp.concatenate(
        [routed[pl.ds(q * PER_PEER + TD, TD), :] for q in range(PEERS)], axis=0
    )
    paired[:, pl.ds(0, SLOTS)] = dot_tn(for_atm.astype(BF16), slot_map[...])[:M]

    for side in range(2):
        halo_copy(side).wait_recv()

    def neighbour(own_tiles, first, rows, index):
        if index < 0:
            return halo_in[1, index + 2, pl.ds(first, rows), :].astype(F32)
        if index >= TD:
            return halo_in[0, index - TD, pl.ds(first, rows), :].astype(F32)
        return own_tiles[index]

    def spread(own_tiles, codes, first, rows):
        results = []
        for t in range(TD):
            total = jnp.zeros((rows, M), F32)
            for d in range(5):
                total = total + class_weight(codes[t, d]) * neighbour(
                    own_tiles, first, rows, t + d - 2
                )
            results.append(total)
        for t in range(TD):
            own_tiles[t] = results[t]

    spread(vert_a, acls, 0, ROWS_A)
    spread(vert_o, ocls, ROWS_A, ROWS_O)

    wide = lax.broadcasted_iota(jnp.int32, (BLOCK, BLOCK * M), 1)
    tall = lax.broadcasted_iota(jnp.int32, (BLOCK, BLOCK * M), 0)
    diagonal = (wide >= tall * M) & (wide < tall * M + M)

    def out_block(anom, vert, out, t, first, scale):
        rows = vert[t, pl.ds(first, BLOCK), :]
        wide_rows = jnp.where(diagonal, jnp.concatenate([rows] * BLOCK, axis=1), 0.0)
        value = dot(wide_rows.astype(BF16), anom[t, pl.ds(first, BLOCK)].reshape(BLOCK * M, C))
        out[pl.ds(first, BLOCK), t, :] = value * scale

    for t in range(TD):
        wet = sea[t].astype(F32)

        def atm_second(b, carry, t=t):
            out_block(atm, vert_a, aout, t, jnp.minimum(b * BLOCK, LA - BLOCK), 1.0)
            return carry

        def ocn_second(b, carry, t=t, wet=wet):
            out_block(ocn, vert_o, oout, t, jnp.minimum(b * BLOCK, LO - BLOCK), wet)
            return carry

        lax.fori_loop(0, pl.cdiv(LA, BLOCK), atm_second, 0)
        lax.fori_loop(0, pl.cdiv(LO, BLOCK), ocn_second, 0)

    for t in range(TD):
        wet = sea[t].astype(F32)
        own_pair = paired[:, pl.ds(t * C, C)]
        for s in range(KA):
            cross = jnp.sum(atm[t, SURF + s].astype(F32) * own_pair, axis=0, keepdims=True)
            aout[SURF + s, pl.ds(t, 1), :] += cross * (COUPLING * RISE[s])
        own_pair = paired[:, pl.ds((TD + t) * C, C)]
        for o in range(KO):
            cross = jnp.sum(ocn[t, o].astype(F32) * own_pair, axis=0, keepdims=True)
            oout[o, pl.ds(t, 1), :] += cross * (COUPLING * FALL[o]) * wet

    for side in range(2):
        halo_copy(side).wait_send()


def local(atm_anom, ocn_anom, atm_vec, ocn_vec, atm_to_ocean, sea_tiles, atm_class, ocn_class):
    hbm = pl.BlockSpec(memory_space=pltpu.HBM)
    smem = pl.BlockSpec(memory_space=pltpu.SMEM)
    vmem = pl.BlockSpec(memory_space=pltpu.VMEM)
    dma = pltpu.SemaphoreType.DMA
    atm_out, ocn_out = pl.pallas_call(
        kernel,
        out_shape=(
            jax.ShapeDtypeStruct((LA, TD, C), F32),
            jax.ShapeDtypeStruct((LO, TD, C), F32),
        ),
        in_specs=[hbm] * 5 + [smem] * 3,
        out_specs=(vmem, vmem),
        scratch_shapes=[
            pltpu.VMEM((TD, LA, M, C), BF16),
            pltpu.VMEM((TD, LO, M, C), BF16),
            pltpu.VMEM((LA, TD, C), BF16),
            pltpu.VMEM((LO, TD, C), BF16),
            pltpu.VMEM((TD, C), jnp.int32),
            pltpu.VMEM((LA * TD, C), F32),
            pltpu.VMEM((LO * TD, C), F32),
            pltpu.VMEM((SLOTS, SLOTS), BF16),
            pltpu.VMEM((C, SLOTS), BF16),
            pltpu.VMEM((ROUTE, C), F32),
            pltpu.VMEM((PEERS, PER_PEER, C), BF16),
            pltpu.VMEM((PEERS, PER_PEER, C), BF16),
            pltpu.VMEM((TD, M, C), F32),
            pltpu.VMEM((TD, M, C), F32),
            pltpu.VMEM((TD, ROWS_A, M), F32),
            pltpu.VMEM((TD, ROWS_O, M), F32),
            pltpu.VMEM((2, 2, HALO_ROWS, M), BF16),
            pltpu.VMEM((2, 2, HALO_ROWS, M), BF16),
            pltpu.VMEM((M, 2 * SLOTS), F32),
            dma((2 + 2 * TD,)),
            dma((3,)),
            dma,
            dma,
            dma,
            dma((2,)),
            dma((2,)),
        ],
        compiler_params=pltpu.CompilerParams(
            collective_id=0, has_side_effects=True, vmem_limit_bytes=62 * 1024 * 1024
        ),
    )(
        jnp.transpose(atm_anom, (0, 2, 1, 3)),
        jnp.transpose(ocn_anom, (0, 2, 1, 3)),
        jnp.transpose(atm_vec, (1, 0, 2)),
        jnp.transpose(ocn_vec, (1, 0, 2)),
        atm_to_ocean,
        sea_tiles,
        atm_class,
        ocn_class,
    )
    return jnp.transpose(atm_out, (1, 0, 2)), jnp.transpose(ocn_out, (1, 0, 2))


def solution(mesh):
    both = ("dom", "tile")
    in_specs = (
        P(both, None, None, None),
        P(both, None, None, None),
        P(both, None, None),
        P(both, None, None),
        P(both, None),
        P(both),
        P(both, None),
        P(both, None),
    )
    out_specs = (P(both, None, None), P(both, None, None))
    return jax.shard_map(local, mesh=mesh, in_specs=in_specs, out_specs=out_specs, check_vma=False)
```

time: 63.3 us -> 48.5 us (0.77)
  Pallas kernels: 53.8 us -> 44.4 us
  local copies, waits for them, and re-layouts: 8.58 us -> 3.25 us
    pallas_call x1, Pallas kernels: 53.8 us -> 44.4 us  [local(): pl.pallas_call(kernel, out_shape=(jax.ShapeDtypeStruct((LA, TD, C), F32),...]
    unnamed x16 -> x2, local copies, waits for them, and re-layouts: 8.58 us -> 3.25 us
where the time goes in v2:
time: 48.5 us; the launch traced here: 48.3 us
  Pallas kernels  44.4 us (92%)
  local copies, waits for them, and re-layouts  3.25 us (7%)
  between operations  0.64 us (1%)
    pallas_call x1, Pallas kernels, local(): pl.pallas_call(kernel, out_shape=(jax.ShapeDtypeStruct((LA, TD, C), F32),...  44.4 us
    unnamed x2, local copies, waits for them, and re-layouts  3.25 us

profile of v2, /device:TPU:0, one launch (start us, length us, event | category | flops | bytes accessed | tf_op | source)
XLA Modules:
  0.0 48.3 jit_solution(17853168684294803577)
XLA Ops:
  0.6 44.4 %shard_map.95 = (f32[127,4,128]{2,1,0:T(4,128)}, f32[75,4,128]{2,1,0:T(4,128)}) custom-call(bf16[4,127,80,128]{3,2,1,0:T(8,128)(2,1)} %bitcast.6, bf16[4,75,80,128]{3,2,1,0:T(8,128)(2,1)} %bitcast.7, bf16[127,4,128]{2,1,0:T(4,128)(2,1)} %bitcast.10, bf16[75,4,128]{2,1,0:T(4,128)(2,1)} %bitcast.11, s32[4,128]{1,0:T(4,128)} %pair_hbm.1, s32[4]{0:T(128)} %sea.1, ...), custom_call_target="tpu_custom_call" | custom-call | tf_op jit(solution)/shard_map/pallas_call | solution.py:379
  45.0 1.7 %copy.12 = f32[4,127,128]{2,0,1:T(4,128)} copy(f32[4,127,128]{2,0,1:T(4,128)} %bitcast.8) | data formatting | bytes 520192
  46.7 1.6 %copy.13 = f32[4,75,128]{2,0,1:T(4,128)} copy(f32[4,75,128]{2,0,1:T(4,128)} %bitcast.9) | data formatting | bytes 307200

commit v3 on v2

--- a/solution.py
+++ b/solution.py
@@ -24,8 +24,10 @@
 PER_PEER = 8
 ROUTE = PEERS * PER_PEER
 SLOTS = TD * C
-GROUP = 4
+HALF = BLOCK // 2
 UNROLL = 9
+ATM_BLOCKS = (0, 16, 32, 48, 64, 80, SURF - BLOCK)
+OCN_BLOCKS = (KO, 32, 48, LO - BLOCK)
 
 COUPLING = 8.0
 CLASS_TABLE = (1.0, 0.7, 0.45, 0.25, 0.0)
@@ -79,10 +81,6 @@
 
     lax.fori_loop(0, (PEERS - 1) // UNROLL, several, 0)
     action(wrap(me + PEERS - 1, PEERS))
-
-
-def lanes_sum(x):
-    return jnp.sum(x, axis=1, keepdims=True)
 
 
 def kernel(
@@ -137,9 +135,11 @@
     for_peers(me, greet)
 
     proj_a[pl.ds(M, C - M), :] = jnp.zeros((C - M, SLOTS), BF16)
-    lane = lax.broadcasted_iota(jnp.int32, (1, C), 1)
-    lanes = lax.broadcasted_iota(jnp.int32, (M, C), 1)
-    sub = lax.broadcasted_iota(jnp.int32, (8, C), 0)
+    for t in range(TD):
+        coeff_a[t, pl.ds(ROWS_A - 8, 8), :] = jnp.zeros((8, M), F32)
+        coeff_o[t, pl.ds(ROWS_O - 8, 8), :] = jnp.zeros((8, M), F32)
+    sub_m = lax.broadcasted_iota(jnp.int32, (HALF, M), 0)
+    sub_c = lax.broadcasted_iota(jnp.int32, (HALF, C), 0)
 
     for copy in small_loads():
         copy.wait()
@@ -162,30 +162,39 @@
 
         lax.fori_loop(0, SLOTS // C, one_hot, 0)
 
+    def coeff_block(anom, vec, coeff, t, first):
+        rows = vector_rows(vec, t, first, BLOCK)
+        none = jnp.zeros((HALF, C), F32)
+        left = jnp.concatenate([rows[:HALF], none], axis=0)
+        right = jnp.concatenate([none, rows[HALF:]], axis=0)
+        both = jnp.concatenate([left, right], axis=1).astype(BF16)
+        low = jnp.zeros((HALF, M), F32)
+        high = jnp.zeros((HALF, M), F32)
+        for j in range(HALF):
+            pair = jnp.concatenate([anom[t, first + j], anom[t, first + HALF + j]], axis=1)
+            out = dot_nt(both, pair)
+            low = jnp.where(sub_m == j, out[:HALF], low)
+            high = jnp.where(sub_m == j, out[HALF:], high)
+        coeff[t, pl.ds(first, HALF), :] = low
+        coeff[t, pl.ds(first + HALF, HALF), :] = high
+
     for copy in surface_loads():
         copy.wait()
 
-    def surface(anom, vec, t, first, scale):
+    def project(anom, vec, t, first, scale):
         rows = vector_rows(vec, t, first, KA)
         total = jnp.zeros((M, C), F32)
-        found = jnp.zeros((M, C), F32)
         for s in range(KA):
-            product = anom[t, first + s].astype(F32) * (rows[s : s + 1] * scale[s])
-            total = total + product
-            found = jnp.where(lanes == s, lanes_sum(product), found)
-        undo = jnp.zeros((1, C), F32)
-        for s in range(KA):
-            undo = jnp.where(lane == s, 1.0 / scale[s], undo)
-        return total, found * undo
+            total = total + anom[t, first + s].astype(F32) * (rows[s : s + 1] * scale[s])
+        return total
 
     def surface_tile(t, carry):
         wet = sea[t].astype(F32)
-        total, found = surface(ocn, ovf, t, 0, FALL)
-        coeff_o[t] = found
-        turned = jnp.transpose(total * wet)
+        coeff_block(ocn, ovf, coeff_o, t, 0)
+        coeff_block(atm, avf, coeff_a, t, SURF)
+        turned = jnp.transpose(project(ocn, ovf, t, 0, FALL) * wet)
         routed[pl.ds(TD + t, C, stride=PER_PEER), pl.ds(0, M)] = turned
-        total, found = surface(atm, avf, t, SURF, RISE)
-        coeff_a[t] = pltpu.roll(found, SURF, 1)
+        total = project(atm, avf, t, SURF, RISE)
         proj_a[pl.ds(0, M), pl.ds(pl.multiple_of(t * C, C), C)] = total.astype(BF16)
         return carry
 
@@ -214,78 +223,43 @@
 
     for_peers(me, push)
 
-    def coeff_block(anom, vec, coeff, t, first):
-        rows = vector_rows(vec, t, first, BLOCK)
-        spot = lax.broadcasted_iota(jnp.int32, (BLOCK, C), 0)
-        left = jnp.where(spot < GROUP, rows, 0.0).astype(BF16)
-        right = jnp.where((spot >= GROUP) & (spot < 2 * GROUP), rows, 0.0).astype(BF16)
-        stack = jnp.concatenate(
-            [
-                anom[t, pl.ds(first, GROUP)].reshape(GROUP * M, C),
-                anom[t, pl.ds(first + GROUP, GROUP)].reshape(GROUP * M, C),
-            ],
-            axis=1,
-        )
-        out = dot_nt(stack, jnp.concatenate([left, right], axis=1))
-        out = jnp.concatenate([out, jnp.zeros((GROUP * M, C - BLOCK), F32)], axis=1)
-        found = jnp.zeros((M, C), F32)
-        for g in range(GROUP):
-            found = jnp.where(
-                (lanes == g) | (lanes == g + GROUP), out[g * M : (g + 1) * M], found
-            )
-        for j in range(2 * GROUP, BLOCK):
-            product = anom[t, first + j].astype(F32) * rows[j : j + 1]
-            found = jnp.where(lanes == j, lanes_sum(product), found)
-        moved = pltpu.roll(found, first, 1)
-        here = (lanes >= first) & (lanes < first + BLOCK)
-        coeff[t] = jnp.where(here, moved, coeff[t])
-
     ahigh, alow = taper_split(ROWS_A, LA, 12.0)
-    ohigh, olow = taper_split(C, LO, 8.0)
+    ohigh, olow = taper_split(ROWS_O, LO, 8.0)
 
     def tapered(high, low, value):
         top = value.astype(BF16)
         rest = (value - top.astype(F32)).astype(BF16)
-        return dot_nt(high, top) + dot_nt(high, rest) + dot_nt(low, top)
-
-    def halo_copy(side):
-        step = 31 if side == 0 else 1
+        return dot(high, top) + dot(high, rest) + dot(low, top)
+
+    def halo_copy(t):
+        step = jnp.where(t < TD // 2, 31, 1)
         return pltpu.make_async_remote_copy(
-            src_ref=halo_out.at[side],
-            dst_ref=halo_in.at[side],
-            send_sem=halo_send.at[side],
-            recv_sem=halo_recv.at[side],
+            src_ref=halo_out.at[t],
+            dst_ref=halo_in.at[t],
+            send_sem=halo_send.at[t],
+            recv_sem=halo_recv.at[t],
             device_id=me_dom * 32 + wrap(me_tile + step, 32),
             device_id_type=LOGICAL,
         )
 
     def first_pass(t, carry):
-        def atm_block(b, inner):
-            coeff_block(atm, avf, coeff_a, t, jnp.minimum(b * BLOCK, SURF - BLOCK))
-            return inner
-
-        def ocn_block(b, inner):
-            coeff_block(ocn, ovf, coeff_o, t, KO + jnp.minimum(b * BLOCK, LO - KO - BLOCK))
-            return inner
-
-        lax.fori_loop(0, pl.cdiv(SURF, BLOCK), atm_block, 0)
-        lax.fori_loop(0, pl.cdiv(LO - KO, BLOCK), ocn_block, 0)
+        for copy in tile_loads(t):
+            copy.wait()
+        for first in ATM_BLOCKS:
+            coeff_block(atm, avf, coeff_a, t, first)
+        for first in OCN_BLOCKS:
+            coeff_block(ocn, ovf, coeff_o, t, first)
         wet = sea[t].astype(F32)
         tap_a = tapered(ahigh, alow, coeff_a[t])
-        tap_o = tapered(ohigh[:ROWS_O], olow[:ROWS_O], coeff_o[t]) * wet
+        tap_o = tapered(ohigh, olow, coeff_o[t]) * wet
         vert_a[t] = tap_a
         vert_o[t] = tap_o
-        side, place = t // 2, t % 2
-        halo_out[side, place, pl.ds(0, ROWS_A), :] = tap_a.astype(BF16)
-        halo_out[side, place, pl.ds(ROWS_A, ROWS_O), :] = tap_o.astype(BF16)
+        halo_out[t, pl.ds(0, ROWS_A), pl.ds(0, M)] = tap_a.astype(BF16)
+        halo_out[t, pl.ds(ROWS_A, ROWS_O), pl.ds(0, M)] = tap_o.astype(BF16)
+        halo_copy(t).start()
         return carry
 
-    for side in range(2):
-        for t in (2 * side, 2 * side + 1):
-            for copy in tile_loads(t):
-                copy.wait()
-        lax.fori_loop(2 * side, 2 * side + 2, first_pass, 0)
-        halo_copy(side).start()
+    lax.fori_loop(0, TD, first_pass, 0)
 
     own.wait()
     everyone = pltpu.make_async_remote_copy(
@@ -307,15 +281,13 @@
     )
     paired[:, pl.ds(0, SLOTS)] = dot_tn(for_atm.astype(BF16), slot_map[...])[:M]
 
-    for side in range(2):
-        halo_copy(side).wait_recv()
+    for t in range(TD):
+        halo_copy(t).wait_recv()
 
     def neighbour(own_tiles, first, rows, index):
-        if index < 0:
-            return halo_in[1, index + 2, pl.ds(first, rows), :].astype(F32)
-        if index >= TD:
-            return halo_in[0, index - TD, pl.ds(first, rows), :].astype(F32)
-        return own_tiles[index]
+        if 0 <= index < TD:
+            return own_tiles[index]
+        return halo_in[index % TD, pl.ds(first, rows), pl.ds(0, M)].astype(F32)
 
     def spread(own_tiles, codes, first, rows):
         results = []
@@ -336,39 +308,42 @@
     tall = lax.broadcasted_iota(jnp.int32, (BLOCK, BLOCK * M), 0)
     diagonal = (wide >= tall * M) & (wide < tall * M + M)
 
-    def out_block(anom, vert, out, t, first, scale):
+    def out_block(anom, vert, t, first):
         rows = vert[t, pl.ds(first, BLOCK), :]
         wide_rows = jnp.where(diagonal, jnp.concatenate([rows] * BLOCK, axis=1), 0.0)
-        value = dot(wide_rows.astype(BF16), anom[t, pl.ds(first, BLOCK)].reshape(BLOCK * M, C))
-        out[pl.ds(first, BLOCK), t, :] = value * scale
-
-    for t in range(TD):
+        return dot(wide_rows.astype(BF16), anom[t, pl.ds(first, BLOCK)].reshape(BLOCK * M, C))
+
+    def crossed(anom, t, first, pair, scale):
+        halves = []
+        for half in range(2):
+            found = jnp.zeros((HALF, C), F32)
+            for s in range(HALF):
+                level = half * HALF + s
+                cross = jnp.sum(anom[t, first + level].astype(F32) * pair, axis=0, keepdims=True)
+                found = jnp.where(sub_c == s, cross * (COUPLING * scale[level]), found)
+            halves.append(found)
+        return jnp.concatenate(halves, axis=0)
+
+    def second_pass(t, carry):
         wet = sea[t].astype(F32)
-
-        def atm_second(b, carry, t=t):
-            out_block(atm, vert_a, aout, t, jnp.minimum(b * BLOCK, LA - BLOCK), 1.0)
-            return carry
-
-        def ocn_second(b, carry, t=t, wet=wet):
-            out_block(ocn, vert_o, oout, t, jnp.minimum(b * BLOCK, LO - BLOCK), wet)
-            return carry
-
-        lax.fori_loop(0, pl.cdiv(LA, BLOCK), atm_second, 0)
-        lax.fori_loop(0, pl.cdiv(LO, BLOCK), ocn_second, 0)
-
-    for t in range(TD):
-        wet = sea[t].astype(F32)
-        own_pair = paired[:, pl.ds(t * C, C)]
-        for s in range(KA):
-            cross = jnp.sum(atm[t, SURF + s].astype(F32) * own_pair, axis=0, keepdims=True)
-            aout[SURF + s, pl.ds(t, 1), :] += cross * (COUPLING * RISE[s])
-        own_pair = paired[:, pl.ds((TD + t) * C, C)]
-        for o in range(KO):
-            cross = jnp.sum(ocn[t, o].astype(F32) * own_pair, axis=0, keepdims=True)
-            oout[o, pl.ds(t, 1), :] += cross * (COUPLING * FALL[o]) * wet
-
-    for side in range(2):
-        halo_copy(side).wait_send()
+        pair = paired[:, pl.ds(pl.multiple_of(t * C, C), C)]
+        for first in ATM_BLOCKS[:-1] + (SURF - BLOCK, SURF):
+            value = out_block(atm, vert_a, t, first)
+            if first == SURF:
+                value = value + crossed(atm, t, SURF, pair, RISE)
+            aout[pl.ds(first, BLOCK), t, :] = value
+        pair = paired[:, pl.ds(pl.multiple_of((TD + t) * C, C), C)]
+        for first in (0,) + OCN_BLOCKS:
+            value = out_block(ocn, vert_o, t, first)
+            if first == 0:
+                value = value + crossed(ocn, t, 0, pair, FALL)
+            oout[pl.ds(first, BLOCK), t, :] = value * wet
+        return carry
+
+    lax.fori_loop(0, TD, second_pass, 0)
+
+    for t in range(TD):
+        halo_copy(t).wait_send()
 
 
 def local(atm_anom, ocn_anom, atm_vec, ocn_vec, atm_to_ocean, sea_tiles, atm_class, ocn_class):
@@ -397,20 +372,20 @@
             pltpu.VMEM((ROUTE, C), F32),
             pltpu.VMEM((PEERS, PER_PEER, C), BF16),
             pltpu.VMEM((PEERS, PER_PEER, C), BF16),
-            pltpu.VMEM((TD, M, C), F32),
-            pltpu.VMEM((TD, M, C), F32),
             pltpu.VMEM((TD, ROWS_A, M), F32),
             pltpu.VMEM((TD, ROWS_O, M), F32),
-            pltpu.VMEM((2, 2, HALO_ROWS, M), BF16),
-            pltpu.VMEM((2, 2, HALO_ROWS, M), BF16),
+            pltpu.VMEM((TD, ROWS_A, M), F32),
+            pltpu.VMEM((TD, ROWS_O, M), F32),
+            pltpu.VMEM((TD, HALO_ROWS, C), BF16),
+            pltpu.VMEM((TD, HALO_ROWS, C), BF16),
             pltpu.VMEM((M, 2 * SLOTS), F32),
             dma((2 + 2 * TD,)),
             dma((3,)),
             dma,
             dma,
             dma,
-            dma((2,)),
-            dma((2,)),
+            dma((TD,)),
+            dma((TD,)),
         ],
         compiler_params=pltpu.CompilerParams(
             collective_id=0, has_side_effects=True, vmem_limit_bytes=62 * 1024 * 1024

time: 48.5 us -> 30.3 us (0.62)
  Pallas kernels: 44.4 us -> 26.2 us
    pallas_call x1, Pallas kernels: 44.4 us -> 26.2 us  [local(): pl.pallas_call(kernel, out_shape=(jax.ShapeDtypeStruct((LA, TD, C), F32),...]
where the time goes in v3:
time: 30.3 us; the launch traced here: 30.1 us
  Pallas kernels  26.2 us (86%)
  local copies, waits for them, and re-layouts  3.25 us (11%)
  between operations  0.64 us (2%)
    pallas_call x1, Pallas kernels, local(): pl.pallas_call(kernel, out_shape=(jax.ShapeDtypeStruct((LA, TD, C), F32),...  26.2 us
    unnamed x2, local copies, waits for them, and re-layouts  3.25 us

profile of v3, /device:TPU:0, one launch (start us, length us, event | category | flops | bytes accessed | tf_op | source)
XLA Modules:
  0.0 30.1 jit_solution(17888590990857194343)
XLA Ops:
  0.6 26.2 %shard_map.95 = (f32[127,4,128]{2,1,0:T(4,128)}, f32[75,4,128]{2,1,0:T(4,128)}) custom-call(bf16[4,127,80,128]{3,2,1,0:T(8,128)(2,1)} %bitcast.6, bf16[4,75,80,128]{3,2,1,0:T(8,128)(2,1)} %bitcast.7, bf16[127,4,128]{2,1,0:T(4,128)(2,1)} %bitcast.10, bf16[75,4,128]{2,1,0:T(4,128)(2,1)} %bitcast.11, s32[4,128]{1,0:T(4,128)} %pair_hbm.1, s32[4]{0:T(128)} %sea.1, ...), custom_call_target="tpu_custom_call" | custom-call | tf_op jit(solution)/shard_map/pallas_call | solution.py:354
  26.8 1.7 %copy.12 = f32[4,127,128]{2,0,1:T(4,128)} copy(f32[4,127,128]{2,0,1:T(4,128)} %bitcast.8) | data formatting | bytes 520192
  28.5 1.6 %copy.13 = f32[4,75,128]{2,0,1:T(4,128)} copy(f32[4,75,128]{2,0,1:T(4,128)} %bitcast.9) | data formatting | bytes 307200

commit v4 on v3

--- a/solution.py
+++ b/solution.py
@@ -84,8 +84,8 @@
 
 
 def kernel(
-    atm_hbm, ocn_hbm, avec_hbm, ovec_hbm, pair_hbm, sea, acls, ocls, aout, oout,
-    atm, ocn, avec, ovec, pairing, avf, ovf, slot_map, proj_a, routed, outgoing, incoming,
+    atm_hbm, ocn_hbm, avec_hbm, ovec_hbm, pair_hbm, sea_hbm, acls_hbm, ocls_hbm, aout, oout,
+    atm, ocn, sea, acls, ocls, avec, ovec, pairing, avf, ovf, slot_map, proj_a, routed, outgoing, incoming,
     coeff_a, coeff_o, vert_a, vert_o, halo_out, halo_in, paired,
     load_sems, small_sems, send_sem, recv_sem, own_sem, halo_send, halo_recv,
 ):
@@ -97,6 +97,9 @@
             pltpu.make_async_copy(pair_hbm, pairing, small_sems.at[2]),
             pltpu.make_async_copy(ovec_hbm, ovec, small_sems.at[1]),
             pltpu.make_async_copy(avec_hbm, avec, small_sems.at[0]),
+            pltpu.make_async_copy(sea_hbm, sea, small_sems.at[3]),
+            pltpu.make_async_copy(acls_hbm, acls, small_sems.at[4]),
+            pltpu.make_async_copy(ocls_hbm, ocls, small_sems.at[5]),
         ]
 
     def surface_loads():
@@ -348,20 +351,23 @@
 
 def local(atm_anom, ocn_anom, atm_vec, ocn_vec, atm_to_ocean, sea_tiles, atm_class, ocn_class):
     hbm = pl.BlockSpec(memory_space=pltpu.HBM)
-    smem = pl.BlockSpec(memory_space=pltpu.SMEM)
     vmem = pl.BlockSpec(memory_space=pltpu.VMEM)
     dma = pltpu.SemaphoreType.DMA
+    far = functools.partial(pltpu.with_memory_space_constraint, memory_space=pltpu.HBM)
     atm_out, ocn_out = pl.pallas_call(
         kernel,
         out_shape=(
             jax.ShapeDtypeStruct((LA, TD, C), F32),
             jax.ShapeDtypeStruct((LO, TD, C), F32),
         ),
-        in_specs=[hbm] * 5 + [smem] * 3,
+        in_specs=[hbm] * 8,
         out_specs=(vmem, vmem),
         scratch_shapes=[
             pltpu.VMEM((TD, LA, M, C), BF16),
             pltpu.VMEM((TD, LO, M, C), BF16),
+            pltpu.SMEM((TD,), jnp.int32),
+            pltpu.SMEM((TD, 5), jnp.int32),
+            pltpu.SMEM((TD, 5), jnp.int32),
             pltpu.VMEM((LA, TD, C), BF16),
             pltpu.VMEM((LO, TD, C), BF16),
             pltpu.VMEM((TD, C), jnp.int32),
@@ -380,7 +386,7 @@
             pltpu.VMEM((TD, HALO_ROWS, C), BF16),
             pltpu.VMEM((M, 2 * SLOTS), F32),
             dma((2 + 2 * TD,)),
-            dma((3,)),
+            dma((6,)),
             dma,
             dma,
             dma,
@@ -388,17 +394,17 @@
             dma((TD,)),
         ],
         compiler_params=pltpu.CompilerParams(
-            collective_id=0, has_side_effects=True, vmem_limit_bytes=62 * 1024 * 1024
+            collective_id=0, has_side_effects=True, vmem_limit_bytes=40 * 1024 * 1024
         ),
     )(
-        jnp.transpose(atm_anom, (0, 2, 1, 3)),
-        jnp.transpose(ocn_anom, (0, 2, 1, 3)),
-        jnp.transpose(atm_vec, (1, 0, 2)),
-        jnp.transpose(ocn_vec, (1, 0, 2)),
-        atm_to_ocean,
-        sea_tiles,
-        atm_class,
-        ocn_class,
+        far(jnp.transpose(atm_anom, (0, 2, 1, 3))),
+        far(jnp.transpose(ocn_anom, (0, 2, 1, 3))),
+        far(jnp.transpose(atm_vec, (1, 0, 2))),
+        far(jnp.transpose(ocn_vec, (1, 0, 2))),
+        far(atm_to_ocean),
+        far(sea_tiles),
+        far(atm_class),
+        far(ocn_class),
     )
     return jnp.transpose(atm_out, (1, 0, 2)), jnp.transpose(ocn_out, (1, 0, 2))
 

time: 30.3 us -> 25.2 us (0.83)
  Pallas kernels: 26.2 us -> 23.1 us
  local copies, waits for them, and re-layouts: 3.25 us -> 1.36 us
    pallas_call x1, Pallas kernels: 26.2 us -> 23.1 us  [local(): pl.pallas_call(kernel, out_shape=(jax.ShapeDtypeStruct((LA, TD, C), F32),...]
    unnamed x2, local copies, waits for them, and re-layouts: 3.25 us -> 1.36 us
where the time goes in v4:
time: 25.2 us; the launch traced here: 25.1 us
  Pallas kernels  23.1 us (92%)
  local copies, waits for them, and re-layouts  1.36 us (5%)
  between operations  0.64 us (3%)
    pallas_call x1, Pallas kernels, local(): pl.pallas_call(kernel, out_shape=(jax.ShapeDtypeStruct((LA, TD, C), F32),...  23.1 us
    unnamed x2, local copies, waits for them, and re-layouts  1.36 us

profile of v4, /device:TPU:0, one launch (start us, length us, event | category | flops | bytes accessed | tf_op | source)
XLA Modules:
  0.0 25.1 jit_solution(10344803041249544364)
XLA Ops:
  0.6 23.1 %shard_map.95 = (f32[127,4,128]{2,1,0:T(4,128)S(1)}, f32[75,4,128]{2,1,0:T(4,128)S(1)}) custom-call(bf16[4,127,80,128]{3,2,1,0:T(8,128)(2,1)} %bitcast.8, bf16[4,75,80,128]{3,2,1,0:T(8,128)(2,1)} %bitcast.9, bf16[127,4,128]{2,1,0:T(4,128)(2,1)} %bitcast.10, bf16[75,4,128]{2,1,0:T(4,128)(2,1)} %bitcast.11, s32[4,128]{1,0:T(4,128)} %pair_hbm.1, s32[4]{0:T(128)} %sea_hbm.1, ...), custom_call_target="tpu_custom_call" | custom-call | tf_op jit(solution)/shard_map/pallas_call | solution.py:357
  23.7 0.7 %copy.12 = f32[4,127,128]{2,0,1:T(4,128)} copy(f32[4,127,128]{2,0,1:T(4,128)S(1)} %bitcast.6) | data formatting | bytes 520192
  24.4 0.7 %copy.13 = f32[4,75,128]{2,0,1:T(4,128)} copy(f32[4,75,128]{2,0,1:T(4,128)S(1)} %bitcast.7) | data formatting | bytes 307200

commit v5 on v4

--- a/solution.py
+++ b/solution.py
@@ -86,7 +86,7 @@
 def kernel(
     atm_hbm, ocn_hbm, avec_hbm, ovec_hbm, pair_hbm, sea_hbm, acls_hbm, ocls_hbm, aout, oout,
     atm, ocn, sea, acls, ocls, avec, ovec, pairing, avf, ovf, slot_map, proj_a, routed, outgoing, incoming,
-    coeff_a, coeff_o, vert_a, vert_o, halo_out, halo_in, paired,
+    coeff_a, coeff_o, vert_a, vert_o, halo_out, halo_in, paired, cross_a, cross_o,
     load_sems, small_sems, send_sem, recv_sem, own_sem, halo_send, halo_recv,
 ):
     me_dom, me_tile = lax.axis_index("dom"), lax.axis_index("tile")
@@ -126,9 +126,6 @@
 
     for copy in small_loads() + surface_loads():
         copy.start()
-    for t in range(TD):
-        for copy in tile_loads(t):
-            copy.start()
 
     barrier = pltpu.get_barrier_semaphore()
 
@@ -136,6 +133,8 @@
         pl.semaphore_signal(barrier, inc=1, device_id=peer, device_id_type=LOGICAL)
 
     for_peers(me, greet)
+    for copy in tile_loads(0):
+        copy.start()
 
     proj_a[pl.ds(M, C - M), :] = jnp.zeros((C - M, SLOTS), BF16)
     for t in range(TD):
@@ -183,6 +182,8 @@
 
     for copy in surface_loads():
         copy.wait()
+    for copy in tile_loads(1):
+        copy.start()
 
     def project(anom, vec, t, first, scale):
         rows = vector_rows(vec, t, first, KA)
@@ -248,6 +249,12 @@
     def first_pass(t, carry):
         for copy in tile_loads(t):
             copy.wait()
+
+        @pl.when(t < TD - 2)
+        def _():
+            for copy in tile_loads(t + 2):
+                copy.start()
+
         for first in ATM_BLOCKS:
             coeff_block(atm, avf, coeff_a, t, first)
         for first in OCN_BLOCKS:
@@ -284,6 +291,26 @@
     )
     paired[:, pl.ds(0, SLOTS)] = dot_tn(for_atm.astype(BF16), slot_map[...])[:M]
 
+    def crossed(anom, t, first, pair, scale):
+        halves = []
+        for half in range(2):
+            found = jnp.zeros((HALF, C), F32)
+            for s in range(HALF):
+                level = half * HALF + s
+                cross = jnp.sum(anom[t, first + level].astype(F32) * pair, axis=0, keepdims=True)
+                found = jnp.where(sub_c == s, cross * (COUPLING * scale[level]), found)
+            halves.append(found)
+        return jnp.concatenate(halves, axis=0)
+
+    def cross_tile(t, carry):
+        cols = pl.ds(pl.multiple_of(t * C, C), C)
+        cross_a[t] = crossed(atm, t, SURF, paired[:, cols], RISE)
+        cols = pl.ds(pl.multiple_of((TD + t) * C, C), C)
+        cross_o[t] = crossed(ocn, t, 0, paired[:, cols], FALL)
+        return carry
+
+    lax.fori_loop(0, TD, cross_tile, 0)
+
     for t in range(TD):
         halo_copy(t).wait_recv()
 
@@ -316,30 +343,17 @@
         wide_rows = jnp.where(diagonal, jnp.concatenate([rows] * BLOCK, axis=1), 0.0)
         return dot(wide_rows.astype(BF16), anom[t, pl.ds(first, BLOCK)].reshape(BLOCK * M, C))
 
-    def crossed(anom, t, first, pair, scale):
-        halves = []
-        for half in range(2):
-            found = jnp.zeros((HALF, C), F32)
-            for s in range(HALF):
-                level = half * HALF + s
-                cross = jnp.sum(anom[t, first + level].astype(F32) * pair, axis=0, keepdims=True)
-                found = jnp.where(sub_c == s, cross * (COUPLING * scale[level]), found)
-            halves.append(found)
-        return jnp.concatenate(halves, axis=0)
-
     def second_pass(t, carry):
         wet = sea[t].astype(F32)
-        pair = paired[:, pl.ds(pl.multiple_of(t * C, C), C)]
         for first in ATM_BLOCKS[:-1] + (SURF - BLOCK, SURF):
             value = out_block(atm, vert_a, t, first)
             if first == SURF:
-                value = value + crossed(atm, t, SURF, pair, RISE)
+                value = value + cross_a[t]
             aout[pl.ds(first, BLOCK), t, :] = value
-        pair = paired[:, pl.ds(pl.multiple_of((TD + t) * C, C), C)]
         for first in (0,) + OCN_BLOCKS:
             value = out_block(ocn, vert_o, t, first)
             if first == 0:
-                value = value + crossed(ocn, t, 0, pair, FALL)
+                value = value + cross_o[t]
             oout[pl.ds(first, BLOCK), t, :] = value * wet
         return carry
 
@@ -385,6 +399,8 @@
             pltpu.VMEM((TD, HALO_ROWS, C), BF16),
             pltpu.VMEM((TD, HALO_ROWS, C), BF16),
             pltpu.VMEM((M, 2 * SLOTS), F32),
+            pltpu.VMEM((TD, BLOCK, C), F32),
+            pltpu.VMEM((TD, BLOCK, C), F32),
             dma((2 + 2 * TD,)),
             dma((6,)),
             dma,

time: 25.2 us -> 24.1 us (0.956)
  Pallas kernels: 23.1 us -> 22 us
    pallas_call x1, Pallas kernels: 23.1 us -> 22 us  [local(): pl.pallas_call(kernel, out_shape=(jax.ShapeDtypeStruct((LA, TD, C), F32),...]
where the time goes in v5:
time: 24.1 us; the launch traced here: 24 us
  Pallas kernels  22 us (91%)
  local copies, waits for them, and re-layouts  1.36 us (6%)
  between operations  0.64 us (3%)
    pallas_call x1, Pallas kernels, local(): pl.pallas_call(kernel, out_shape=(jax.ShapeDtypeStruct((LA, TD, C), F32),...  22 us
    unnamed x2, local copies, waits for them, and re-layouts  1.36 us

profile of v5, /device:TPU:0, one launch (start us, length us, event | category | flops | bytes accessed | tf_op | source)
XLA Modules:
  0.0 24.0 jit_solution(5947800054267624596)
XLA Ops:
  0.6 22.0 %shard_map.95 = (f32[127,4,128]{2,1,0:T(4,128)S(1)}, f32[75,4,128]{2,1,0:T(4,128)S(1)}) custom-call(bf16[4,127,80,128]{3,2,1,0:T(8,128)(2,1)} %bitcast.8, bf16[4,75,80,128]{3,2,1,0:T(8,128)(2,1)} %bitcast.9, bf16[127,4,128]{2,1,0:T(4,128)(2,1)} %bitcast.10, bf16[75,4,128]{2,1,0:T(4,128)(2,1)} %bitcast.11, s32[4,128]{1,0:T(4,128)} %pair_hbm.1, s32[4]{0:T(128)} %sea_hbm.1, ...), custom_call_target="tpu_custom_call" | custom-call | tf_op jit(solution)/shard_map/pallas_call | solution.py:371
  22.6 0.7 %copy.12 = f32[4,127,128]{2,0,1:T(4,128)} copy(f32[4,127,128]{2,0,1:T(4,128)S(1)} %bitcast.6) | data formatting | bytes 520192
  23.3 0.7 %copy.13 = f32[4,75,128]{2,0,1:T(4,128)} copy(f32[4,75,128]{2,0,1:T(4,128)S(1)} %bitcast.7) | data formatting | bytes 307200
